TPU v7x, 32 devices: a whole 2x2x4 slice. The times are simulated.
32 devices in a mesh: scen: 8 (over z, y), area: 4 (over x, core).
Axes of the slice: x: 2, y: 2, z: 4, core: 2. Of those that a mesh axis runs over, the one named last changes fastest.
Arguments:
- wind: bfloat16 [8, 24, 24576], P('scen', None, 'area'), may hold values from -4 to 4
- load: bfloat16 [24, 24576], P(None, 'area'), may hold values from 0 to 1.5
- ptdf_tiles: bfloat16 [128, 32, 128, 128], P('area'), may hold values from -0.09375 to 0.09375
- tile_cols: int32 [128, 32], P('area'), may hold values from 0 to 191, as said below
- line_cap: float32 [16384], P('area'), may hold values from 0.3 to 3
- gen_bus: int32 [4096], P('area'), may hold values from 0 to 24575, as said below
- gen_data: float32 [4, 4096], P(None, 'area'), may hold values from 0.05 to 18, as said below
- prob_weight: int32 [8], P('scen'), may hold values from 1 to 16
Outputs:
- commit_mean: float32 [24, 4096], P(None, 'area')
- dispatch_mean: float32 [24, 4096], P(None, 'area')
- dispatch: float32 [8, 24, 4096], P('scen', None, 'area')
- line_flow: float32 [8, 24, 16384], P('scen', None, 'area')
Inputs may be any that keep to these rules, and one draw needn't show every extreme that they name: `tile_cols`: the 32 bus tiles of one row of line tiles are distinct. `gen_bus`: generator g stands at a bus of area g // 1024, that is among buses (g // 1024) * 6144 to (g // 1024 + 1) * 6144 - 1. `gen_data`: linear cost 0.5 to 2, quadratic cost 0.05 to 0.5, commitment cost 0.2 to 1, capacity 2 to 18.
All inputs are finite; a program needn't handle non-finite values.
Results may differ from a plain program's by a relative error of at most 0.003.
Values may be sent and summed in bfloat16 or wider, within the bound.
A program may use at most 128 MiB of HBM per device.

v0:
```python
import jax
import jax.numpy as jnp
from jax import lax
from jax.sharding import PartitionSpec as P

BUSES = 24576
ITERS = 2
STEPS = 2


penalty = 1.0
flow_weight = 0.25
commit_step = 0.5


def on_device(wind, load, ptdf_tiles, tile_cols, line_cap, gen_bus, gen_data, prob_weight):
    scen_local, hours, bus_local = wind.shape
    gen_local = gen_bus.shape[0]
    tile = ptdf_tiles.shape[2]
    rows = scen_local * hours
    first_bus = lax.axis_index("area") * bus_local
    onehot = (
        gen_bus[:, None] - first_bus == jnp.arange(bus_local, dtype=jnp.int32)[None, :]
    ).astype(jnp.float32)
    linear = gen_data[0][None, :]
    quadratic = gen_data[1][None, :]
    fixed_cost = gen_data[2][None, :]
    capacity = gen_data[3][None, :]
    step_gen = 1.0 / (quadratic + penalty + 2.0)
    outside = (wind.astype(jnp.float32) - load.astype(jnp.float32)[None]).reshape(rows, bus_local)
    total = lax.psum(jnp.sum(prob_weight.astype(jnp.float32)), "scen")
    probs = jnp.repeat(prob_weight.astype(jnp.float32) / total, hours)[:, None]
    commit = jnp.full((rows, gen_local), 0.5, jnp.float32)
    dispatch = jnp.zeros((rows, gen_local), jnp.float32) + 0.25 * capacity
    comm_mean = jnp.full((hours, gen_local), 0.5, jnp.float32)
    disp_mean = jnp.zeros((hours, gen_local), jnp.float32) + 0.25 * capacity
    w_comm = jnp.zeros((rows, gen_local), jnp.float32)
    w_disp = jnp.zeros((rows, gen_local), jnp.float32)
    flow = jnp.zeros((rows, line_cap.shape[0]), jnp.float32)
    for round_index in range(ITERS):
        comm_rows = jnp.tile(comm_mean, (scen_local, 1))
        disp_rows = jnp.tile(disp_mean, (scen_local, 1))
        for step_index in range(STEPS):
            placed = jnp.dot(
                dispatch,
                onehot,
                precision=lax.Precision.HIGHEST,
                preferred_element_type=jnp.float32,
            )
            injection = (placed + outside).astype(jnp.bfloat16)
            whole = lax.all_gather(injection, "area", axis=1, tiled=True)
            picked = whole.reshape(rows, -1, tile)[:, tile_cols]
            flow = jnp.einsum(
                "rkzb,kzlb->rkl", picked, ptdf_tiles, preferred_element_type=jnp.float32
            ).reshape(rows, -1)
            excess = (flow - jnp.clip(flow, -line_cap, line_cap)).astype(jnp.bfloat16)
            imbalance = lax.psum(jnp.sum(injection.astype(jnp.float32), axis=1), "area")
            contrib = jnp.einsum(
                "rkl,kzlb->rkzb",
                excess.reshape(rows, -1, tile),
                ptdf_tiles,
                preferred_element_type=jnp.float32,
            )
            partial_value = (
                jnp.zeros((rows, whole.shape[1] // tile, tile), jnp.float32)
                .at[:, tile_cols]
                .add(contrib)
            )
            partial_value = partial_value.reshape(rows, -1)
            price_bus = lax.psum_scatter(
                partial_value.astype(jnp.bfloat16), "area", scatter_dimension=1, tiled=True
            ).astype(jnp.float32)
            price_gen = jnp.dot(
                price_bus,
                onehot.T,
                precision=lax.Precision.HIGHEST,
                preferred_element_type=jnp.float32,
            )
            grad = (
                linear
                + quadratic * dispatch
                + flow_weight * price_gen
                + imbalance[:, None] / BUSES
                + w_disp
                + penalty * (dispatch - disp_rows)
            )
            commit = jnp.clip(
                commit
                - commit_step
                * (fixed_cost - dispatch / capacity + w_comm + penalty * (commit - comm_rows)),
                0.0,
                1.0,
            )
            dispatch = jnp.clip(dispatch - step_gen * grad, 0.0, capacity * commit)
        comm_term = jnp.sum((probs * commit).reshape(scen_local, hours, gen_local), axis=0)
        disp_term = jnp.sum((probs * dispatch).reshape(scen_local, hours, gen_local), axis=0)
        comm_mean, disp_mean = lax.psum((comm_term, disp_term), "scen")
        w_comm = w_comm + penalty * (commit - jnp.tile(comm_mean, (scen_local, 1)))
        w_disp = w_disp + penalty * (dispatch - jnp.tile(disp_mean, (scen_local, 1)))
    return (
        comm_mean,
        disp_mean,
        dispatch.reshape(scen_local, hours, gen_local),
        flow.reshape(scen_local, hours, -1),
    )


def solution(mesh):
    placed = (
        P("scen", None, "area"),
        P(None, "area"),
        P("area", None, None, None),
        P("area", None),
        P("area"),
        P("area"),
        P(None, "area"),
        P("scen"),
    )
    return jax.shard_map(
        on_device,
        mesh=mesh,
        in_specs=placed,
        out_specs=(
            P(None, "area"),
            P(None, "area"),
            P("scen", None, "area"),
            P("scen", None, "area"),
        ),
        check_vma=False,
    )
```

profile of v0, /device:TPU:0, one launch (start us, length us, event | category | flops | bytes accessed | tf_op | source)
XLA Modules:
  0.0 857.9 jit_solution(6121021990289339343)
XLA Ops:
  7.2 0.9 add_divide_fusion
  8.1 0.7 broadcast_subtract_fusion
  8.8 9.9 %convert_reduce_fusion.3 = (f32[24]{0:T(128)S(1)}, bf16[24,6144]{1,0:T(8,128)(2,1)}) fusion(bf16[24,6144]{1,0:T(8,128)(2,1)} %param.9, bf16[1,24,6144]{2,1,0:T(8,128)(2,1)} %param.8, s32[1024]{0:T(1024)S(1)} %broadcast_subtract_fusion, f32[1024]{0:T(1024)S(1)} %bitcast.239), kind=kOutput, calls=%fused_computation.88 | convolution fusion | flops 1819262976 | bytes 893024 | tf_op jit(solution)/shard_map/dot_general | solution.py:44
  19.3 19.7 %all-gather.5.cloned.1.call-done = bf16[24,24576]{1,0:T(8,128)(2,1)} async-done(((bf16[24,6144]{1,0:T(8,128)(2,1)}), bf16[24,24576]{1,0:T(8,128)(2,1)}) %all-gather.5.cloned.1.call-update) | async-done | bytes 1179664 | tf_op jit(solution)/shard_map/all_gather | solution.py:51
  39.0 1.5 copy_bitcast_fusion.7
  40.5 9.2 %gather_fusion = bf16[1024,24,128]{2,1,0:T(8,128)(2,1)} fusion(bf16[24,192,128]{2,0,1:T(8,128)(2,1)S(1)} %copy_bitcast_fusion.7, s32[1024]{0:T(1024)S(1)} %broadcast_clamp_fusion), kind=kCustom, calls=%fused_computation | custom fusion | bytes 12587008 | tf_op jit(solution)/shard_map/gather | solution.py:52
  49.7 33.8 %fusion.73 = f32[32,24,32,128]{3,1,2,0:T(8,128)} fusion(bf16[32,32,128,128]{3,2,1,0:T(8,128)(2,1)} %param.10, bf16[24,32,32,128]{3,0,2,1:T(8,128)(2,1)} %bitcast.215, f32[32,128]{1,0:T(8,128)S(1)} %negate_bitcast_fusion, f32[32,128]{1,0:T(8,128)S(1)} %bitcast.218), kind=kOutput, calls=%fused_computation.126 | convolution fusion | flops 1611005952 | bytes 52461568 | tf_op jit(solution)/shard_map/rkl,kzlb->rkzb/dot_general | solution.py:58
  83.7 86.4 %scatter_fusion = f32[24,192,128]{2,0,1:T(8,128)S(1)} fusion(f32[24,192,128]{2,0,1:T(8,128)S(1)} %broadcast.83.clone, s32[1024]{0:T(1024)S(1)} %reshape.144, f32[1024,24,128]{2,1,0:T(8,128)} %bitcast.210), kind=kCustom, calls=%fused_computation.4 | custom fusion | flops 3145728 | bytes 37752832 | tf_op jit(solution)/shard_map/scatter-add | solution.py:67
  170.2 1.1 copy_bitcast_fusion.3
  172.0 21.9 %psum.63 = f32[1]{0:T(128)} all-reduce(f32[1]{0:T(128)S(6)} %convert_element_type.77), channel_id=1, replica_groups=mesh['scen'=8,'area'=4] {'scen'}, use_global_device_ids=true, to_apply=%region_0.0 | all-reduce | flops 1 | bytes 8 | tf_op jit(solution)/shard_map/psum | solution.py:31
  194.6 5.9 psum.64
  200.6 6.3 broadcast_multiply_fusion.3
  206.9 9.0 %convert_reduce_fusion.2 = (f32[24]{0:T(128)S(1)}, bf16[24,6144]{1,0:T(8,128)(2,1)}) fusion(bf16[24,6144]{1,0:T(8,128)(2,1)S(1)} %copy-done.3, bf16[1,24,6144]{2,1,0:T(8,128)(2,1)S(1)} %copy-done.4, f32[24,1024]{1,0:T(8,128)S(1)} %get-tuple-element.25, s32[1024]{0:T(1024)S(1)} %broadcast_subtract_fusion), kind=kOutput, calls=%fused_computation.87 | convolution fusion | flops 1819262976 | bytes 987232 | tf_op jit(solution)/shard_map/dot_general | solution.py:44
  216.0 14.1 %all-gather.7.cloned.1.call-done = bf16[24,24576]{1,0:T(8,128)(2,1)} async-done(((bf16[24,6144]{1,0:T(8,128)(2,1)}), bf16[24,24576]{1,0:T(8,128)(2,1)}) %all-gather.7.cloned.1.call-update) | async-done | bytes 1179664 | tf_op jit(solution)/shard_map/all_gather | solution.py:51
  230.1 1.5 copy_bitcast_fusion.6
  231.6 9.2 %gather_fusion.1 = bf16[1024,24,128]{2,1,0:T(8,128)(2,1)} fusion(bf16[24,192,128]{2,0,1:T(8,128)(2,1)S(1)} %copy_bitcast_fusion.6, s32[1024]{0:T(1024)S(1)} %broadcast_clamp_fusion), kind=kCustom, calls=%fused_computation.1 | custom fusion | bytes 12587008 | tf_op jit(solution)/shard_map/gather | solution.py:52
  240.8 33.8 %fusion.74 = f32[32,24,32,128]{3,1,2,0:T(8,128)} fusion(bf16[32,32,128,128]{3,2,1,0:T(8,128)(2,1)} %param.10, bf16[24,32,32,128]{3,0,2,1:T(8,128)(2,1)} %bitcast.216, f32[32,128]{1,0:T(8,128)S(1)} %negate_bitcast_fusion, f32[32,128]{1,0:T(8,128)S(1)} %bitcast.219), kind=kOutput, calls=%fused_computation.127 | convolution fusion | flops 1611005952 | bytes 52461568 | tf_op jit(solution)/shard_map/rkl,kzlb->rkzb/dot_general | solution.py:58
  274.8 86.4 %scatter_fusion.1 = f32[24,192,128]{2,0,1:T(8,128)S(1)} fusion(f32[24,192,128]{2,0,1:T(8,128)S(1)} %broadcast.83.clone.1, s32[1024]{0:T(1024)S(1)} %reshape.144, f32[1024,24,128]{2,1,0:T(8,128)} %bitcast.211), kind=kCustom, calls=%fused_computation.5 | custom fusion | flops 3145728 | bytes 37752832 | tf_op jit(solution)/shard_map/scatter-add | solution.py:67
  361.3 1.1 copy_bitcast_fusion.2
  362.5 5.9 psum.65
  368.3 19.8 %reduce-scatter.7.cloned.1.call-done = bf16[24,6144]{1,0:T(8,128)(2,1)} async-done(((bf16[24,24576]{1,0:T(8,128)(2,1)}), bf16[24,6144]{1,0:T(8,128)(2,1)}) %reduce-scatter.7.cloned.1.call-update) | async-done | bytes 294928 | tf_op jit(solution)/shard_map/reduce_scatter | solution.py:70
  388.2 6.3 broadcast_multiply_fusion.2
  394.5 9.2 %convert_reduce_fusion.1 = (f32[24]{0:T(128)S(1)}, bf16[24,6144]{1,0:T(8,128)(2,1)}) fusion(bf16[24,6144]{1,0:T(8,128)(2,1)S(1)} %copy-done.3, bf16[1,24,6144]{2,1,0:T(8,128)(2,1)S(1)} %copy-done.5, f32[24,1024]{1,0:T(8,128)S(1)} %get-tuple-element.29, s32[1024]{0:T(1024)S(1)} %broadcast_subtract_fusion), kind=kOutput, calls=%fused_computation.86 | convolution fusion | flops 1819262976 | bytes 987232 | tf_op jit(solution)/shard_map/dot_general | solution.py:44
  404.4 17.0 %all-gather.9.cloned.1.call-done = bf16[24,24576]{1,0:T(8,128)(2,1)} async-done(((bf16[24,6144]{1,0:T(8,128)(2,1)}), bf16[24,24576]{1,0:T(8,128)(2,1)}) %all-gather.9.cloned.1.call-update) | async-done | bytes 1179664 | tf_op jit(solution)/shard_map/all_gather | solution.py:51
  421.4 1.5 copy_bitcast_fusion.5
  422.8 9.2 %gather_fusion.2 = bf16[1024,24,128]{2,1,0:T(8,128)(2,1)} fusion(bf16[24,192,128]{2,0,1:T(8,128)(2,1)S(1)} %copy_bitcast_fusion.5, s32[1024]{0:T(1024)S(1)} %broadcast_clamp_fusion), kind=kCustom, calls=%fused_computation.2 | custom fusion | bytes 12587008 | tf_op jit(solution)/shard_map/gather | solution.py:52
  432.0 33.8 %fusion.75 = f32[32,24,32,128]{3,1,2,0:T(8,128)} fusion(bf16[32,32,128,128]{3,2,1,0:T(8,128)(2,1)} %param.10, bf16[24,32,32,128]{3,0,2,1:T(8,128)(2,1)} %bitcast.217, f32[32,128]{1,0:T(8,128)S(1)} %negate_bitcast_fusion, f32[32,128]{1,0:T(8,128)S(1)} %bitcast.220), kind=kOutput, calls=%fused_computation.128 | convolution fusion | flops 1611005952 | bytes 52461568 | tf_op jit(solution)/shard_map/rkl,kzlb->rkzb/dot_general | solution.py:58
  466.1 86.4 %scatter_fusion.2 = f32[24,192,128]{2,0,1:T(8,128)S(1)} fusion(f32[24,192,128]{2,0,1:T(8,128)S(1)} %broadcast.83.clone.2, s32[1024]{0:T(1024)S(1)} %reshape.144, f32[1024,24,128]{2,1,0:T(8,128)} %bitcast.212), kind=kCustom, calls=%fused_computation.6 | custom fusion | flops 3145728 | bytes 37752832 | tf_op jit(solution)/shard_map/scatter-add | solution.py:67
  552.5 1.1 copy_bitcast_fusion.1
  553.7 5.9 psum.67
  559.6 0.9 sub.130
  560.5 18.9 %reduce-scatter.9.cloned.1.call-done = bf16[24,6144]{1,0:T(8,128)(2,1)} async-done(((bf16[24,24576]{1,0:T(8,128)(2,1)}), bf16[24,6144]{1,0:T(8,128)(2,1)}) %reduce-scatter.9.cloned.1.call-update) | async-done | bytes 294928 | tf_op jit(solution)/shard_map/reduce_scatter | solution.py:70
  579.4 6.5 broadcast_multiply_fusion.1
  585.9 8.8 %convert_reduce_fusion = (f32[24]{0:T(128)S(1)}, bf16[24,6144]{1,0:T(8,128)(2,1)}) fusion(bf16[24,6144]{1,0:T(8,128)(2,1)S(1)} %copy-done.3, bf16[1,24,6144]{2,1,0:T(8,128)(2,1)S(1)} %copy-done.6, f32[24,1024]{1,0:T(8,128)S(1)} %get-tuple-element.32, s32[1024]{0:T(1024)S(1)} %broadcast_subtract_fusion), kind=kOutput, calls=%fused_computation.85 | convolution fusion | flops 1819262976 | bytes 987232 | tf_op jit(solution)/shard_map/dot_general | solution.py:44
  594.8 17.5 %all-gather.11.cloned.1.call-done = bf16[24,24576]{1,0:T(8,128)(2,1)} async-done(((bf16[24,6144]{1,0:T(8,128)(2,1)}), bf16[24,24576]{1,0:T(8,128)(2,1)}) %all-gather.11.cloned.1.call-update) | async-done | bytes 1179664 | tf_op jit(solution)/shard_map/all_gather | solution.py:51
  612.4 1.5 copy_bitcast_fusion.4
  613.9 9.3 %gather_fusion.3 = bf16[1024,24,128]{2,1,0:T(8,128)(2,1)} fusion(bf16[24,192,128]{2,0,1:T(8,128)(2,1)S(1)} %copy_bitcast_fusion.4, s32[1024]{0:T(1024)S(1)} %broadcast_clamp_fusion), kind=kCustom, calls=%fused_computation.3 | custom fusion | bytes 12587008 | tf_op jit(solution)/shard_map/gather | solution.py:52
  623.2 15.9 %convolution_bitcast_fusion = f32[24,32,128]{2,0,1:T(8,128)S(1)} fusion(bf16[24,32,32,128]{3,0,2,1:T(8,128)(2,1)} %bitcast.214, bf16[32,32,128,128]{3,2,1,0:T(8,128)(2,1)} %param.10), kind=kOutput, calls=%fused_computation.33 | convolution fusion | flops 805306368 | bytes 40239104 | tf_op jit(solution)/shard_map/rkzb,kzlb->rkl/dot_general | solution.py:53
  639.1 17.8 %fusion.63 = f32[32,24,32,128]{3,1,2,0:T(8,128)} fusion(bf16[32,32,128,128]{3,2,1,0:T(8,128)(2,1)} %param.10, f32[24,32,128]{2,0,1:T(8,128)S(1)} %convolution_bitcast_fusion, f32[32,128]{1,0:T(8,128)S(1)} %negate_bitcast_fusion, f32[32,128]{1,0:T(8,128)S(1)} %bitcast.221), kind=kOutput, calls=%fused_computation.97 | convolution fusion | flops 805699584 | bytes 46563328 | tf_op jit(solution)/shard_map/rkl,kzlb->rkzb/dot_general | solution.py:58
  657.0 86.4 %scatter_fusion.3 = f32[24,192,128]{2,0,1:T(8,128)S(1)} fusion(f32[24,192,128]{2,0,1:T(8,128)S(1)} %broadcast.83, s32[1024]{0:T(1024)S(1)} %reshape.144, f32[1024,24,128]{2,1,0:T(8,128)} %bitcast.213), kind=kCustom, calls=%fused_computation.7 | custom fusion | flops 3145728 | bytes 37752832 | tf_op jit(solution)/shard_map/scatter-add | solution.py:67
  743.5 1.1 copy_bitcast_fusion
  744.7 5.9 psum.70
  750.5 19.8 %reduce-scatter.11.cloned.1.call-done = bf16[24,6144]{1,0:T(8,128)(2,1)} async-done(((bf16[24,24576]{1,0:T(8,128)(2,1)}), bf16[24,6144]{1,0:T(8,128)(2,1)}) %reduce-scatter.11.cloned.1.call-update) | async-done | bytes 294928 | tf_op jit(solution)/shard_map/reduce_scatter | solution.py:70
  770.4 6.4 broadcast_multiply_fusion
  776.9 0.8 reshape_reshape.3
  777.7 70.1 %all-reduce.5.cloned.1.call-done = (f32[24,1024]{1,0:T(8,128)}, f32[24,1024]{1,0:T(8,128)}) async-done(((f32[24,1024]{1,0:T(8,128)}, f32[24,1024]{1,0:T(8,128)}), (f32[24,1024]{1,0:T(8,128)}, f32[24,1024]{1,0:T(8,128)})) %all-reduce.5.cloned.1.call-update) | async-done | bytes 196624 | tf_op jit(solution)/shard_map/psum | solution.py:97
  847.8 1.5 copy.58
  849.4 1.5 copy.59
  (55 shorter events, 2.5 us)
Async XLA Ops:
  7.2 12.1 %copy-start.2 = (s32[32,32]{1,0:T(8,128)S(1)}, s32[32,32]{1,0:T(8,128)}, u32[]{:S(2)}) copy-start(s32[32,32]{1,0:T(8,128)} %param.11) | copy-start | bytes 12292
  7.2 12.2 %copy-start = (f32[4096]{0:T(1024)S(1)}, f32[4096]{0:T(1024)}, u32[]{:S(2)}) copy-start(f32[4096]{0:T(1024)} %param.12) | copy-start | bytes 49156
  7.2 31.8 %all-gather.5.cloned.1.call-start = ((), (), s32[]{:S(2)}) async-start(), calls=%async_computation.4 | async-start | bytes 1474560 | tf_op jit(solution)/shard_map/all_gather | solution.py:51
  18.7 181.9 %reduce-scatter.5.cloned.1.call-start = ((), (), s32[]{:S(2)}) async-start(), calls=%async_computation.5 | async-start | bytes 1474560 | tf_op jit(solution)/shard_map/reduce_scatter | solution.py:70
  170.1 36.8 %copy-start.3 = (bf16[24,6144]{1,0:T(8,128)(2,1)S(1)}, bf16[24,6144]{1,0:T(8,128)(2,1)}, u32[]{:S(2)}) copy-start(bf16[24,6144]{1,0:T(8,128)(2,1)} %param.9) | copy-start | bytes 884740
  170.2 36.8 %copy-start.4 = (bf16[1,24,6144]{2,1,0:T(8,128)(2,1)S(1)}, bf16[1,24,6144]{2,1,0:T(8,128)(2,1)}, u32[]{:S(2)}) copy-start(bf16[1,24,6144]{2,1,0:T(8,128)(2,1)} %param.8) | copy-start | bytes 884740
  171.3 58.8 %all-gather.7.cloned.1.call-start = ((), (), s32[]{:S(2)}) async-start(), calls=%async_computation.6 | async-start | bytes 1474560 | tf_op jit(solution)/shard_map/all_gather | solution.py:51
  206.9 181.3 %copy-start.7 = (f32[24,1024]{1,0:T(8,128)}, f32[24,1024]{1,0:T(8,128)S(1)}, u32[]{:S(2)}) copy-start(f32[24,1024]{1,0:T(8,128)S(1)} %get-tuple-element.25) | copy-start | bytes 294916
  216.0 172.2 %reduce-scatter.7.cloned.1.call-start = ((), (), s32[]{:S(2)}) async-start(), calls=%async_computation.7 | async-start | bytes 1474560 | tf_op jit(solution)/shard_map/reduce_scatter | solution.py:70
  362.4 32.1 %copy-start.5 = (bf16[1,24,6144]{2,1,0:T(8,128)(2,1)S(1)}, bf16[1,24,6144]{2,1,0:T(8,128)(2,1)}, u32[]{:S(2)}) copy-start(bf16[1,24,6144]{2,1,0:T(8,128)(2,1)} %param.8) | copy-start | bytes 884740
  362.4 59.0 %all-gather.9.cloned.1.call-start = ((), (), s32[]{:S(2)}) async-start(), calls=%async_computation.8 | async-start | bytes 1474560 | tf_op jit(solution)/shard_map/all_gather | solution.py:51
  403.8 155.8 %all-reduce.7.cloned.1.call-start = ((), (), s32[]{:S(2)}) async-start(), calls=%async_computation.13 | async-start | bytes 393216 | tf_op jit(solution)/shard_map/psum | solution.py:97
  404.4 175.1 %reduce-scatter.9.cloned.1.call-start = ((), (), s32[]{:S(2)}) async-start(), calls=%async_computation.9 | async-start | bytes 1474560 | tf_op jit(solution)/shard_map/reduce_scatter | solution.py:70
  466.0 113.4 %copy-start.8 = (f32[24,1024]{1,0:T(8,128)S(1)}, f32[24,1024]{1,0:T(8,128)}, u32[]{:S(2)}) copy-start(f32[24,1024]{1,0:T(8,128)} %copy-done.7) | copy-start | bytes 294916
  553.6 32.3 %copy-start.6 = (bf16[1,24,6144]{2,1,0:T(8,128)(2,1)S(1)}, bf16[1,24,6144]{2,1,0:T(8,128)(2,1)}, u32[]{:S(2)}) copy-start(bf16[1,24,6144]{2,1,0:T(8,128)(2,1)} %param.8) | copy-start | bytes 884740
  553.7 58.7 %all-gather.11.cloned.1.call-start = ((), (), s32[]{:S(2)}) async-start(), calls=%async_computation.10 | async-start | bytes 1474560 | tf_op jit(solution)/shard_map/all_gather | solution.py:51
  594.8 175.6 %reduce-scatter.11.cloned.1.call-start = ((), (), s32[]{:S(2)}) async-start(), calls=%async_computation.11 | async-start | bytes 1474560 | tf_op jit(solution)/shard_map/reduce_scatter | solution.py:70
  657.0 113.4 %copy-start.1 = (f32[24,1024]{1,0:T(8,128)S(1)}, f32[24,1024]{1,0:T(8,128)}, u32[]{:S(2)}) copy-start(f32[24,1024]{1,0:T(8,128)} %get-tuple-element.7) | copy-start | bytes 294916
  744.6 103.2 %all-reduce.5.cloned.1.call-start = ((), (), s32[]{:S(2)}) async-start(), calls=%async_computation.12 | async-start | bytes 393216 | tf_op jit(solution)/shard_map/psum | solution.py:97
Sparse Core Ops, SparseCore 0:
  18.8 20.1 all-gather.4
  171.4 25.6 reduce-scatter.4
  216.1 14.0 all-gather.6
  362.5 25.6 reduce-scatter.6
  403.9 17.4 all-gather.8
  425.2 70.8 all-reduce.6
  553.8 25.6 reduce-scatter.8
  594.9 17.4 all-gather.10
  744.7 25.6 reduce-scatter.10
  776.9 70.8 all-reduce.4
where the time goes:
time: 871 us; the launch traced here: 858 us
  other arithmetic  353 us (41%)
  matrix products  198 us (23%)
  waiting for transfers between devices  198 us (23%)
  local copies, waits for them, and re-layouts  47.5 us (5%)
  blocking collectives  45.4 us (5%)
  between operations  15.9 us (2%)
    scatter-add x4, other arithmetic, on_device(): partial_value = jnp.zeros((rows, whole.shape[1] // tile, tile), jnp.float...  346 us
    dot_general x4, matrix products, on_device(): jnp.einsum('rkl,kzlb->rkzb', excess.reshape(rows, -1, tile), ptdf_tiles,...  119 us
    psum x2, waiting for transfers between devices, on_device(): comm_mean, disp_mean = lax.psum((comm_term, disp_term), 'scen')  70.1 us
    all_gather x4, waiting for transfers between devices, on_device(): whole = lax.all_gather(injection, 'area', axis=1, tiled=True)  68.3 us
    reduce_scatter x4, waiting for transfers between devices, on_device(): lax.psum_scatter(partial_value.astype(jnp.bfloat16), 'area', scatter_dime...  58.6 us
    gather x4, local copies, waits for them, and re-layouts, on_device(): picked = whole.reshape(rows, -1, tile)[:, tile_cols]  36.9 us
    dot_general x4, matrix products, on_device(): jnp.dot(dispatch, onehot, precision=lax.Precision.HIGHEST, preferred_elem...  36.9 us
    dot_general x4, matrix products, on_device(): jnp.dot(price_bus, onehot.T, precision=lax.Precision.HIGHEST, preferred_e...  25.6 us
  transfers between devices with their start and end apart: 10, of which 8 were waited for; matrix products, arithmetic and copies ran while one was open for 16% of the time, Pallas kernels for 0%

commit v1 on v0

v1 whole, which is shorter than its diff:
```python
import functools
import jax
import jax.numpy as jnp
from jax import lax
from jax.experimental import pallas as pl
from jax.experimental.pallas import tpu as pltpu
from jax.sharding import PartitionSpec as P

ITERS = 2
STEPS = 2

penalty = 1.0
flow_weight = 0.25
commit_step = 0.5

SPAN = 8
NT = (((1,), (1,)), ((), ()))
HIGH = lax.Precision.HIGHEST


def flow_kernel(cols_sm, lo_sm, hi_sm, inj, w, cap, bus, flow, price, imb, acc):
    step = pl.program_id(0)
    block, slots, tile, _ = w.shape
    tiles = inj.shape[0]

    @pl.when(step == 0)
    def _():
        acc[...] = jnp.zeros_like(acc)

        def add(t, sums):
            return tuple(s + inj[t * 4 + i].astype(jnp.float32) for i, s in enumerate(sums))

        zero = jnp.zeros(imb.shape, jnp.float32)
        parts = lax.fori_loop(0, tiles // 4, add, (zero,) * 4)
        total = parts[0] + parts[1] + parts[2] + parts[3]
        imb[...] = jnp.broadcast_to(jnp.sum(total, axis=1, keepdims=True), imb.shape)

    flows = []
    cols = []
    for kk in range(block):
        base = (step * block + kk) * slots
        own = [cols_sm[base + z] for z in range(slots)]
        picked = jnp.concatenate([inj[c] for c in own], axis=1)
        wide = jnp.concatenate([w[kk, z] for z in range(slots)], axis=1)
        flows.append(lax.dot_general(picked, wide, NT, preferred_element_type=jnp.float32))
        cols.append(own)
    contribs = []
    for kk in range(block):
        value = flows[kk]
        flow[:, kk * tile:(kk + 1) * tile] = value
        limit = cap[0, :, kk * tile:(kk + 1) * tile]
        excess = (value - jnp.clip(value, -limit, limit)).astype(jnp.bfloat16)
        wide = jnp.concatenate([w[kk, z] for z in range(slots)], axis=1)
        contribs.append(jnp.dot(excess, wide, preferred_element_type=jnp.float32))
    for kk in range(block):
        for z in range(slots):
            c = cols[kk][z]
            acc[c] = acc[c] + contribs[kk][:, z * tile:(z + 1) * tile]

    @pl.when(step == pl.num_programs(0) - 1)
    def _():
        def one(j, carry):
            where = jnp.broadcast_to(bus[j], imb.shape)
            own_tile = where // tile
            lane = where - own_tile * tile

            def pick(t, found):
                values = acc[t].astype(jnp.bfloat16).astype(jnp.float32)
                got = jnp.take_along_axis(values, lane, axis=1, mode="promise_in_bounds")
                return jnp.where(own_tile == t, got, found)

            found = jnp.zeros(imb.shape, jnp.float32)
            low = lo_sm[j]
            for i in range(SPAN):
                found = pick(jnp.minimum(low + i, tiles - 1), found)
            found = lax.fori_loop(low + SPAN, hi_sm[j] + 1, pick, found)
            price[j] = found.astype(jnp.bfloat16)
            return carry

        lax.fori_loop(0, bus.shape[0], one, 0)


def flows_and_prices(inj, w, cols, cap, bus, low, high, block=2):
    tiles, rows, tile = inj.shape
    lines, slots = w.shape[0], w.shape[1]
    block = block if lines % block == 0 else 1
    groups = bus.shape[0]
    return pl.pallas_call(
        flow_kernel,
        grid_spec=pltpu.PrefetchScalarGridSpec(
            num_scalar_prefetch=3,
            grid=(lines // block,),
            in_specs=[
                pl.BlockSpec((tiles, rows, tile), lambda k, *_: (0, 0, 0)),
                pl.BlockSpec((block, slots, tile, tile), lambda k, *_: (k, 0, 0, 0)),
                pl.BlockSpec((1, 1, block * tile), lambda k, *_: (k, 0, 0)),
                pl.BlockSpec((groups, 1, tile), lambda k, *_: (0, 0, 0)),
            ],
            out_specs=[
                pl.BlockSpec((rows, block * tile), lambda k, *_: (0, k)),
                pl.BlockSpec((groups, rows, tile), lambda k, *_: (0, 0, 0)),
                pl.BlockSpec((rows, tile), lambda k, *_: (0, 0)),
            ],
            scratch_shapes=[pltpu.VMEM((tiles, rows, tile), jnp.float32)],
        ),
        out_shape=[
            jax.ShapeDtypeStruct((rows, lines * tile), jnp.float32),
            jax.ShapeDtypeStruct((groups, rows, tile), jnp.bfloat16),
            jax.ShapeDtypeStruct((rows, tile), jnp.float32),
        ],
        compiler_params=pltpu.CompilerParams(vmem_limit_bytes=48 * 2**20),
        name="flow_step",
    )(cols.reshape(-1), low, high, inj, w, cap.reshape(-1, 1, block * tile), bus)


def inject_kernel(lo_sm, hi_sm, slow_sm, disp, bus, wind, load, inj, split):
    chunks, rows, tile = disp.shape
    tiles = inj.shape[0]
    for c in range(chunks):
        value = disp[c]
        first = value.astype(jnp.bfloat16).astype(jnp.float32)
        second = (value - first).astype(jnp.bfloat16).astype(jnp.float32)
        third = value - first - second
        split[c] = jnp.concatenate([first, second, third], axis=0).astype(jnp.bfloat16)

    def folded(sums):
        return sums[:rows] + sums[rows:2 * rows] + sums[2 * rows:]

    def outside(lanes):
        return wind[:, lanes].astype(jnp.float32) - load[:, lanes].astype(jnp.float32)

    for t in range(tiles):
        c = lo_sm[t]
        buses = lax.broadcasted_iota(jnp.int32, (tile, 2 * tile), 0) + t * tile
        here = jnp.concatenate([bus[c], bus[c + 1]], axis=1)
        onehot = jnp.where(buses == here, 1.0, 0.0).astype(jnp.bfloat16)
        left = jnp.concatenate([split[c], split[c + 1]], axis=1)
        sums = lax.dot_general(left, onehot, NT, preferred_element_type=jnp.float32)
        placed = folded(sums) + outside(slice(t * tile, (t + 1) * tile))
        inj[t] = placed.astype(jnp.bfloat16)

    @pl.when(slow_sm[0] > 0)
    def _():
        def one(t, carry):
            buses = lax.broadcasted_iota(jnp.int32, (tile, tile), 0) + t * tile

            def more(c, sums):
                onehot = jnp.where(buses == bus[c], 1.0, 0.0).astype(jnp.bfloat16)
                return sums + lax.dot_general(split[c], onehot, NT, preferred_element_type=jnp.float32)

            zero = jnp.zeros((3 * rows, tile), jnp.float32)
            sums = lax.fori_loop(lo_sm[t], hi_sm[t] + 1, more, zero)
            lanes = pl.ds(pl.multiple_of(t * tile, tile), tile)
            inj[t] = (folded(sums) + outside(lanes)).astype(jnp.bfloat16)
            return carry

        lax.fori_loop(0, tiles, one, 0)


def injected(disp, bus, wind, load, low, high, slow):
    chunks, rows, tile = disp.shape
    tiles = low.shape[0]
    smem = pl.BlockSpec(memory_space=pltpu.SMEM)
    vmem = pl.BlockSpec(memory_space=pltpu.VMEM)
    return pl.pallas_call(
        inject_kernel,
        in_specs=[smem] * 3 + [vmem] * 4,
        out_specs=vmem,
        out_shape=jax.ShapeDtypeStruct((tiles, rows, tile), jnp.bfloat16),
        scratch_shapes=[pltpu.VMEM((chunks, 3 * rows, tile), jnp.bfloat16)],
        name="inject",
    )(low, high, slow, disp, bus, wind, load)


def on_device(areas, wind, load, ptdf_tiles, tile_cols, line_cap, gen_bus, gen_data, prob_weight):
    scen_local, hours, bus_local = wind.shape
    gens = gen_bus.shape[0]
    tile = ptdf_tiles.shape[2]
    rows = scen_local * hours
    chunks = gens // tile
    tiles = bus_local // tile
    buses = bus_local * areas
    first_bus = lax.axis_index("area") * bus_local

    index = jnp.arange(gens, dtype=jnp.int32)
    ahead = (gen_bus[None, :] < gen_bus[:, None]) | (
        (gen_bus[None, :] == gen_bus[:, None]) & (index[None, :] < index[:, None])
    )
    rank = jnp.sum(ahead.astype(jnp.int32), axis=1)
    order = (rank[:, None] == index[None, :]).astype(jnp.float32)
    per_gen = jnp.concatenate([gen_data, gen_bus.astype(jnp.float32)[None]], axis=0)
    per_gen = jnp.dot(per_gen, order, precision=HIGH, preferred_element_type=jnp.float32)
    bus_sorted = jnp.round(per_gen[4]).astype(jnp.int32)
    data = per_gen[:4].reshape(4, chunks, 1, tile)
    linear, quadratic, fixed_cost, capacity = data[0], data[1], data[2], data[3]
    step_gen = 1.0 / (quadratic + penalty + 2.0)

    bus_local_sorted = bus_sorted - first_bus
    starts = jnp.sum(
        (bus_local_sorted[None, :] < (jnp.arange(tiles + 1, dtype=jnp.int32) * tile)[:, None]).astype(jnp.int32), axis=1
    )
    low = jnp.minimum(starts[:-1] // tile, chunks - 2)
    high = (starts[1:] - 1) // tile
    slow = jnp.any(high > low + 1).astype(jnp.int32)[None]
    bus_chunks = bus_local_sorted.reshape(chunks, 1, tile)

    bus_all = lax.all_gather(bus_sorted, "area", axis=0, tiled=True).reshape(-1, 1, tile)
    group_low = bus_all[:, 0, 0] // tile
    group_high = bus_all[:, 0, -1] // tile

    total = lax.psum(jnp.sum(prob_weight.astype(jnp.float32)), "scen")
    probs = jnp.repeat(prob_weight.astype(jnp.float32) / total, hours)[None, :, None]

    shape = (chunks, rows, tile)
    commit = jnp.full(shape, 0.5, jnp.float32)
    dispatch = jnp.zeros(shape, jnp.float32) + 0.25 * capacity
    comm_mean = jnp.full((chunks, hours, tile), 0.5, jnp.float32)
    disp_mean = jnp.zeros((chunks, hours, tile), jnp.float32) + 0.25 * capacity
    w_comm = jnp.zeros(shape, jnp.float32)
    w_disp = jnp.zeros(shape, jnp.float32)
    wind_rows = wind.reshape(rows, bus_local)
    load_rows = jnp.tile(load, (scen_local, 1))
    flow = None
    for round_index in range(ITERS):
        comm_rows = jnp.tile(comm_mean, (1, scen_local, 1))
        disp_rows = jnp.tile(disp_mean, (1, scen_local, 1))
        for step_index in range(STEPS):
            injection = injected(dispatch, bus_chunks, wind_rows, load_rows, low, high, slow)
            whole = lax.all_gather(injection, "area", axis=0, tiled=True)
            flow, partial_price, imbalance = flows_and_prices(
                whole, ptdf_tiles, tile_cols, line_cap, bus_all, group_low, group_high
            )
            pieces = lax.all_to_all(
                partial_price.reshape(areas, chunks, rows, tile), "area", 0, 0
            )
            price_gen = jnp.sum(pieces.astype(jnp.float32), axis=0)
            grad = (
                linear
                + quadratic * dispatch
                + flow_weight * price_gen
                + imbalance[None] / buses
                + w_disp
                + penalty * (dispatch - disp_rows)
            )
            commit = jnp.clip(
                commit
                - commit_step
                * (fixed_cost - dispatch / capacity + w_comm + penalty * (commit - comm_rows)),
                0.0,
                1.0,
            )
            dispatch = jnp.clip(dispatch - step_gen * grad, 0.0, capacity * commit)
        both = jnp.stack([probs * commit, probs * dispatch])
        both = jnp.sum(both.reshape(2, chunks, scen_local, hours, tile), axis=2)
        comm_mean, disp_mean = lax.psum(both, "scen")
        w_comm = w_comm + penalty * (commit - jnp.tile(comm_mean, (1, scen_local, 1)))
        w_disp = w_disp + penalty * (dispatch - jnp.tile(disp_mean, (1, scen_local, 1)))

    outs = jnp.concatenate([comm_mean, disp_mean, dispatch], axis=1)
    outs = jnp.moveaxis(outs, 0, 1).reshape(-1, gens)
    outs = lax.dot_general(
        outs, order, NT, precision=HIGH, preferred_element_type=jnp.float32
    )
    return (
        outs[:hours],
        outs[hours:2 * hours],
        outs[2 * hours:].reshape(scen_local, hours, gens),
        flow.reshape(scen_local, hours, -1),
    )


def solution(mesh):
    placed = (
        P("scen", None, "area"),
        P(None, "area"),
        P("area", None, None, None),
        P("area", None),
        P("area"),
        P("area"),
        P(None, "area"),
        P("scen"),
    )
    return jax.shard_map(
        functools.partial(on_device, mesh.shape["area"]),
        mesh=mesh,
        in_specs=placed,
        out_specs=(
            P(None, "area"),
            P(None, "area"),
            P("scen", None, "area"),
            P("scen", None, "area"),
        ),
        check_vma=False,
    )
```

time: 871 us -> 381 us (0.44); the launches traced: 858 us -> 378 us
  other arithmetic: 353 us -> 10.7 us
  matrix products: 198 us -> 4.47 us
  Pallas kernels: 0 us -> 130 us
  local copies, waits for them, and re-layouts: 47.5 us -> 10.2 us
  waiting for transfers between devices: 198 us -> 165 us
  blocking collectives: 45.4 us -> 28.1 us
  starting transfers between devices: 0.87 us -> 13.7 us
    scatter-add x4 -> x0, other arithmetic: 346 us -> none  [on_device(): partial_value = jnp.zeros((rows, whole.shape[1] // tile, tile), jnp.float...]
    dot_general x13 -> x2, matrix products: 198 us -> 4.47 us  [the longest x1 2.3 us: on_device(): lax.dot_general(outs, order, NT, precision=HIGH, preferred_element_type=j...]
    pallas_call x0 -> x8, Pallas kernels: none -> 130 us  [the longest x4 117 us: flows_and_prices(): pl.pallas_call(flow_kernel, grid_spec=pltpu.PrefetchScalarGridSpec(num_sc...]
    reduce_scatter x4 -> x0, waiting for transfers between devices: 58.6 us -> none  [on_device(): lax.psum_scatter(partial_value.astype(jnp.bfloat16), 'area', scatter_dime...]
    gather x4 -> x0, local copies, waits for them, and re-layouts: 36.9 us -> none  [on_device(): picked = whole.reshape(rows, -1, tile)[:, tile_cols]]
    psum x2, waiting for transfers between devices: 70.1 us -> 98.9 us  [on_device(): comm_mean, disp_mean = lax.psum(both, 'scen')]
    psum x4 -> x0, blocking collectives: 23.6 us -> none  [on_device(): imbalance = lax.psum(jnp.sum(injection.astype(jnp.float32), axis=1), 'area')]
    all_gather x4, waiting for transfers between devices: 68.3 us -> 45.1 us  [on_device(): whole = lax.all_gather(injection, 'area', axis=0, tiled=True)]
  transfers between devices with their start and end apart: 10 -> 10, of which waited for: 8 -> 9; matrix products, arithmetic and copies ran while one was open for 16% -> 1% of each run, Pallas kernels for 0% -> 8%
where the time goes in v1:
time: 381 us; the launch traced here: 378 us
  waiting for transfers between devices  165 us (43%)
  Pallas kernels  130 us (34%)
  blocking collectives  28.1 us (7%)
  between operations  16.2 us (4%)
  starting transfers between devices  13.7 us (4%)
  other arithmetic  10.7 us (3%)
  local copies, waits for them, and re-layouts  10.2 us (3%)
  matrix products  4.47 us (1%)
    pallas_call x4, Pallas kernels, flows_and_prices(): pl.pallas_call(flow_kernel, grid_spec=pltpu.PrefetchScalarGridSpec(num_sc...  117 us
    psum x2, waiting for transfers between devices, on_device(): comm_mean, disp_mean = lax.psum(both, 'scen')  98.9 us
    all_gather x4, waiting for transfers between devices, on_device(): whole = lax.all_gather(injection, 'area', axis=0, tiled=True)  45.1 us
    psum x1, blocking collectives, on_device(): total = lax.psum(jnp.sum(prob_weight.astype(jnp.float32)), 'scen')  21.9 us
    all_to_all x4, waiting for transfers between devices, on_device(): lax.all_to_all(partial_price.reshape(areas, chunks, rows, tile), 'area',...  20.8 us
    all_to_all x4, starting transfers between devices, on_device(): lax.all_to_all(partial_price.reshape(areas, chunks, rows, tile), 'area',...  13.5 us
    pallas_call x4, Pallas kernels, injected(): pl.pallas_call(inject_kernel, in_specs=[smem] * 3 + [vmem] * 4, out_specs...  12.4 us
  transfers between devices with their start and end apart: 10, of which 9 were waited for; matrix products, arithmetic and copies ran while one was open for 1% of the time, Pallas kernels for 8%

profile of v1, /device:TPU:0, one launch (start us, length us, event | category | flops | bytes accessed | tf_op | source)
XLA Modules:
  0.0 378.1 jit_solution(13011959104293312406)
XLA Ops:
  7.2 1.6 convert_reduce_fusion
  8.8 0.7 convert_element_type.43
  9.5 2.2 fusion.1
  11.7 0.6 fusion.63.bus
  12.3 0.2 convert_reduce_fusion.5
  12.5 1.2 compare_reduce_fusion
  14.5 0.6 add.436.disp
  15.1 3.1 inject.4
  18.2 0.8 reshape.284.cols_sm
  19.0 6.2 %all-gather = s32[1,4096]{1,0:T(1,128)S(1)} all-gather(s32[1,1024]{1,0:T(1,128)S(1)} %get-tuple-element.39), channel_id=2, replica_groups=mesh['scen'=8,'area'=4] {'area'}, dimensions={1}, use_global_device_ids=true | all-gather | bytes 20480 | tf_op jit(solution)/shard_map/all_gather | solution.py:207
  25.2 1.3 slice_reduce_fusion
  26.5 12.0 %all-gather.6.cloned.1.call-done.inj = bf16[192,24,128]{2,1,0:T(8,128)(2,1)} async-done(((bf16[48,24,128]{2,1,0:T(8,128)(2,1)}), bf16[192,24,128]{2,1,0:T(8,128)(2,1)}) %all-gather.6.cloned.1.call-update) | async-done | bytes 1179664 | tf_op jit(solution)/shard_map/all_gather | solution.py:229
  38.5 1.3 copy-done.1
  39.8 0.7 copy-done.4
  40.5 29.3 %flow_step.4 = (f32[24,4096]{1,0:T(8,128)}, bf16[32,24,128]{2,1,0:T(8,128)(2,1)}, f32[24,128]{1,0:T(8,128)S(1)}) custom-call(s32[1024]{0:T(1024)S(1)} %reshape.284.cols_sm, s32[32]{0:T(128)S(1)} %get-tuple-element.49.lo_sm, s32[32]{0:T(128)S(1)} %get-tuple-element.48.hi_sm, bf16[192,24,128]{2,1,0:T(8,128)(2,1)S(1)} %copy-done.1, ...), custom_call_target="tpu_custom_call" | custom-call | tf_op jit(solution)/shard_map/flow_step/pallas_call | solution.py:88
  69.8 3.4 all-to-all-start
  73.3 5.2 %all-to-all-done = bf16[4,8,24,128]{3,2,1,0:T(8,128)(2,1)S(1)} async-done(((bf16[4,8,24,128]{3,2,1,0:T(8,128)(2,1)}), bf16[4,8,24,128]{3,2,1,0:T(8,128)(2,1)S(1)}, u32[]{:S(2)}, u32[]{:S(2)}) %all-to-all-start) | async-done | bytes 196640 | tf_op jit(solution)/shard_map/all_to_all | solution.py:233
  78.5 0.7 maximum_minimum_fusion.1.disp
  79.2 3.1 inject.5
  82.3 17.6 %all-gather.8.cloned.1.call-done.inj = bf16[192,24,128]{2,1,0:T(8,128)(2,1)} async-done(((bf16[48,24,128]{2,1,0:T(8,128)(2,1)}), bf16[192,24,128]{2,1,0:T(8,128)(2,1)}) %all-gather.8.cloned.1.call-update) | async-done | bytes 1179664 | tf_op jit(solution)/shard_map/all_gather | solution.py:229
  99.9 1.3 copy-done.3
  101.2 29.3 %flow_step.5 = (f32[24,4096]{1,0:T(8,128)}, bf16[32,24,128]{2,1,0:T(8,128)(2,1)}, f32[24,128]{1,0:T(8,128)S(1)}) custom-call(s32[1024]{0:T(1024)S(1)} %reshape.284.cols_sm, s32[32]{0:T(128)S(1)} %get-tuple-element.49.lo_sm, s32[32]{0:T(128)S(1)} %get-tuple-element.48.hi_sm, bf16[192,24,128]{2,1,0:T(8,128)(2,1)S(1)} %copy-done.3, ...), custom_call_target="tpu_custom_call" | custom-call | tf_op jit(solution)/shard_map/flow_step/pallas_call | solution.py:88
  130.5 3.4 all-to-all-start.1
  133.9 5.2 %all-to-all-done.1 = bf16[4,8,24,128]{3,2,1,0:T(8,128)(2,1)S(1)} async-done(((bf16[4,8,24,128]{3,2,1,0:T(8,128)(2,1)}), bf16[4,8,24,128]{3,2,1,0:T(8,128)(2,1)S(1)}, u32[]{:S(2)}, u32[]{:S(2)}) %all-to-all-start.1) | async-done | bytes 196640 | tf_op jit(solution)/shard_map/all_to_all | solution.py:233
  139.2 0.7 maximum_minimum_fusion.disp
  139.9 3.1 inject.6
  143.7 21.9 %psum.21 = f32[1]{0:T(128)} all-reduce(f32[1]{0:T(128)S(6)} %convert_element_type.42), channel_id=1, replica_groups=mesh['scen'=8,'area'=4] {'scen'}, use_global_device_ids=true, to_apply=%region_0.0 | all-reduce | flops 1 | bytes 8 | tf_op jit(solution)/shard_map/psum | solution.py:211
  166.3 0.7 pad_maximum_fusion
  167.1 1.3 copy-done
  168.3 29.4 %flow_step.6 = (f32[24,4096]{1,0:T(8,128)}, bf16[32,24,128]{2,1,0:T(8,128)(2,1)}, f32[24,128]{1,0:T(8,128)S(1)}) custom-call(s32[1024]{0:T(1024)S(1)} %reshape.284.cols_sm, s32[32]{0:T(128)S(1)} %get-tuple-element.49.lo_sm, s32[32]{0:T(128)S(1)} %get-tuple-element.48.hi_sm, bf16[192,24,128]{2,1,0:T(8,128)(2,1)S(1)} %copy-done, bf16[32,32,128,128]{3,2,1,0:T(8,128)(2,1)} %w.7, ...), custom_call_target="tpu_custom_call" | custom-call | tf_op jit(solution)/shard_map/flow_step/pallas_call | solution.py:88
  197.7 3.4 all-to-all-start.2
  201.1 5.2 %all-to-all-done.2 = bf16[4,8,24,128]{3,2,1,0:T(8,128)(2,1)S(1)} async-done(((bf16[4,8,24,128]{3,2,1,0:T(8,128)(2,1)}), bf16[4,8,24,128]{3,2,1,0:T(8,128)(2,1)S(1)}, u32[]{:S(2)}, u32[]{:S(2)}) %all-to-all-start.2) | async-done | bytes 196640 | tf_op jit(solution)/shard_map/all_to_all | solution.py:233
  206.4 28.3 %all-reduce.3.cloned.1.call-done = f32[2,8,24,128]{3,2,1,0:T(8,128)} async-done(((f32[2,8,24,128]{3,2,1,0:T(8,128)}), f32[2,8,24,128]{3,2,1,0:T(8,128)}) %all-reduce.3.cloned.1.call-update) | async-done | bytes 196624 | tf_op jit(solution)/shard_map/psum | solution.py:255
  234.6 1.7 fusion.21.disp
  236.3 3.2 inject.7
  239.6 1.2 broadcast_multiply_fusion
  240.8 15.5 %all-gather.12.cloned.1.call-done.inj = bf16[192,24,128]{2,1,0:T(8,128)(2,1)} async-done(((bf16[48,24,128]{2,1,0:T(8,128)(2,1)}), bf16[192,24,128]{2,1,0:T(8,128)(2,1)}) %all-gather.12.cloned.1.call-update) | async-done | bytes 1179664 | tf_op jit(solution)/shard_map/all_gather | solution.py:229
  256.2 1.3 copy-done.2
  257.5 29.3 %flow_step.7 = (f32[24,4096]{1,0:T(8,128)}, bf16[32,24,128]{2,1,0:T(8,128)(2,1)}, f32[24,128]{1,0:T(8,128)S(1)}) custom-call(s32[1024]{0:T(1024)S(1)} %reshape.284.cols_sm, s32[32]{0:T(128)S(1)} %get-tuple-element.49.lo_sm, s32[32]{0:T(128)S(1)} %get-tuple-element.48.hi_sm, bf16[192,24,128]{2,1,0:T(8,128)(2,1)S(1)} %copy-done.2, ...), custom_call_target="tpu_custom_call" | custom-call | tf_op jit(solution)/shard_map/flow_step/pallas_call | solution.py:88
  286.8 3.4 all-to-all-start.3
  290.3 5.2 %all-to-all-done.3 = bf16[4,8,24,128]{3,2,1,0:T(8,128)(2,1)S(1)} async-done(((bf16[4,8,24,128]{3,2,1,0:T(8,128)(2,1)}), bf16[4,8,24,128]{3,2,1,0:T(8,128)(2,1)S(1)}, u32[]{:S(2)}, u32[]{:S(2)}) %all-to-all-start.3) | async-done | bytes 196640 | tf_op jit(solution)/shard_map/all_to_all | solution.py:233
  295.5 0.2 fusion.29
  295.8 0.7 pad_maximum_fusion.1
  296.5 0.2 fusion.34
  296.7 70.7 %all-reduce.5.cloned.1.call-done = f32[2,8,24,128]{3,2,1,0:T(8,128)} async-done(((f32[2,8,24,128]{3,2,1,0:T(8,128)}), f32[2,8,24,128]{3,2,1,0:T(8,128)}) %all-reduce.5.cloned.1.call-update) | async-done | bytes 196624 | tf_op jit(solution)/shard_map/psum | solution.py:255
  367.3 1.0 slice_bitcast_fusion.2
  368.3 2.3 fusion
  370.6 0.7 slice_bitcast_fusion
  (41 shorter events, 0.7 us)
Async XLA Ops:
  7.2 31.3 %all-gather.6.cloned.1.call-start = ((), (), s32[]{:S(2)}) async-start(), calls=%async_computation.4 | async-start | bytes 1474560 | tf_op jit(solution)/shard_map/all_gather | solution.py:229
  38.5 1.3 copy-start.1
  39.8 0.7 copy-start.4
  40.5 59.4 %copy-start.5 = (f32[4096]{0:T(1024)S(1)}, f32[4096]{0:T(1024)}, u32[]{:S(2)}) copy-start(f32[4096]{0:T(1024)} %param.12) | copy-start | bytes 49156
  69.8 8.6 %all-to-all-start = ((bf16[4,8,24,128]{3,2,1,0:T(8,128)(2,1)}), bf16[4,8,24,128]{3,2,1,0:T(8,128)(2,1)S(1)}, u32[]{:S(2)}, u32[]{:S(2)}) async-start(bf16[4,8,24,128]{3,2,1,0:T(8,128)(2,1)} %bitcast.12), calls=%async_computation | async-start | bytes 393216 | tf_op jit(solution)/shard_map/all_to_all | solution.py:233
  73.2 26.7 %all-gather.8.cloned.1.call-start = ((), (), s32[]{:S(2)}) async-start(), calls=%async_computation.5 | async-start | bytes 1474560 | tf_op jit(solution)/shard_map/all_gather | solution.py:229
  99.9 1.3 copy-start.3
  130.5 8.6 %all-to-all-start.1 = ((bf16[4,8,24,128]{3,2,1,0:T(8,128)(2,1)}), bf16[4,8,24,128]{3,2,1,0:T(8,128)(2,1)S(1)}, u32[]{:S(2)}, u32[]{:S(2)}) async-start(bf16[4,8,24,128]{3,2,1,0:T(8,128)(2,1)} %bitcast.14), calls=%async_computation.1 | async-start | bytes 393216 | tf_op jit(solution)/shard_map/all_to_all | solution.py:233
  133.9 33.2 %all-gather.10.cloned.1.call-start = ((), (), s32[]{:S(2)}) async-start(), calls=%async_computation.7 | async-start | bytes 1474560 | tf_op jit(solution)/shard_map/all_gather | solution.py:229
  143.0 91.6 %all-reduce.3.cloned.1.call-start = ((), (), s32[]{:S(2)}) async-start(), calls=%async_computation.6 | async-start | bytes 393216 | tf_op jit(solution)/shard_map/psum | solution.py:255
  167.0 1.3 copy-start
  168.3 66.3 %copy-start.7 = (f32[8,24,128]{2,1,0:T(8,128)S(1)}, f32[8,24,128]{2,1,0:T(8,128)}, u32[]{:S(2)}) copy-start(f32[8,24,128]{2,1,0:T(8,128)} %maximum_minimum_fusion.disp) | copy-start | bytes 294916
  197.7 8.6 %all-to-all-start.2 = ((bf16[4,8,24,128]{3,2,1,0:T(8,128)(2,1)}), bf16[4,8,24,128]{3,2,1,0:T(8,128)(2,1)S(1)}, u32[]{:S(2)}, u32[]{:S(2)}) async-start(bf16[4,8,24,128]{3,2,1,0:T(8,128)(2,1)} %bitcast.16), calls=%async_computation.2 | async-start | bytes 393216 | tf_op jit(solution)/shard_map/all_to_all | solution.py:233
  201.1 55.1 %all-gather.12.cloned.1.call-start = ((), (), s32[]{:S(2)}) async-start(), calls=%async_computation.8 | async-start | bytes 1474560 | tf_op jit(solution)/shard_map/all_gather | solution.py:229
  256.2 1.3 copy-start.2
  257.5 38.0 %copy-start.6 = (f32[2,8,24,128]{3,2,1,0:T(8,128)S(1)}, f32[2,8,24,128]{3,2,1,0:T(8,128)}, u32[]{:S(2)}) copy-start(f32[2,8,24,128]{3,2,1,0:T(8,128)} %all-reduce.3.cloned.1.call-done) | copy-start | bytes 589828
  257.5 39.0 %copy-start.8 = (f32[8,24,128]{2,1,0:T(8,128)S(1)}, f32[8,24,128]{2,1,0:T(8,128)}, u32[]{:S(2)}) copy-start(f32[8,24,128]{2,1,0:T(8,128)} %fusion.21.disp) | copy-start | bytes 294916
  286.8 8.6 %all-to-all-start.3 = ((bf16[4,8,24,128]{3,2,1,0:T(8,128)(2,1)}), bf16[4,8,24,128]{3,2,1,0:T(8,128)(2,1)S(1)}, u32[]{:S(2)}, u32[]{:S(2)}) async-start(bf16[4,8,24,128]{3,2,1,0:T(8,128)(2,1)} %bitcast.20), calls=%async_computation.3 | async-start | bytes 393216 | tf_op jit(solution)/shard_map/all_to_all | solution.py:233
  290.2 77.1 %all-reduce.5.cloned.1.call-start = ((), (), s32[]{:S(2)}) async-start(), calls=%async_computation.9 | async-start | bytes 393216 | tf_op jit(solution)/shard_map/psum | solution.py:255
Sparse Core Ops, SparseCore 0:
  18.3 20.1 all-gather.5
  82.4 17.4 all-gather.7
  143.1 17.4 all-gather.9
  167.1 67.4 all-reduce.2
  239.7 16.4 all-gather.11
  296.6 70.6 all-reduce.4

commit v2 on v1

--- a/solution.py
+++ b/solution.py
@@ -172,7 +172,153 @@
     )(low, high, slow, disp, bus, wind, load)
 
 
-def on_device(areas, wind, load, ptdf_tiles, tile_cols, line_cap, gen_bus, gen_data, prob_weight):
+MESH = pl.DeviceIdType.MESH
+VMEM = pl.BlockSpec(memory_space=pltpu.VMEM)
+
+
+def greet(axis, peers):
+    barrier = pltpu.get_barrier_semaphore()
+    for peer in peers:
+        pl.semaphore_signal(barrier, inc=1, device_id={axis: peer}, device_id_type=MESH)
+    pl.semaphore_wait(barrier, len(peers))
+
+
+def sent(axis, peer, src, dst, send, recv):
+    copy = pltpu.make_async_remote_copy(
+        src_ref=src, dst_ref=dst, send_sem=send, recv_sem=recv, device_id={axis: peer}, device_id_type=MESH
+    )
+    copy.start()
+    return copy
+
+
+def remote(kernel, out, args, sems, scratch, ident, name):
+    return pl.pallas_call(
+        kernel,
+        in_specs=[VMEM] * len(args),
+        out_specs=VMEM,
+        out_shape=out,
+        scratch_shapes=list(scratch) + [pltpu.SemaphoreType.DMA((k,)) for k in sems],
+        compiler_params=pltpu.CompilerParams(collective_id=ident, has_side_effects=True),
+        name=name,
+    )(*args)
+
+
+def gather_kernel(axis, n, x, out, send, recv):
+    me = lax.axis_index(axis)
+    peers = [lax.rem(me + i, n) for i in range(1, n)]
+    greet(axis, peers)
+    copies = [sent(axis, peer, x, out.at[me], send.at[i], recv.at[i]) for i, peer in enumerate(peers)]
+    out[me] = x[...]
+    for copy in copies:
+        copy.wait()
+
+
+def gathered(x, axis, n, ident):
+    out = jax.ShapeDtypeStruct((n,) + x.shape, x.dtype)
+    return remote(functools.partial(gather_kernel, axis, n), out, [x], [n - 1] * 2, [], ident, "gather")
+
+
+def exchange_kernel(axis, n, x, out, landed, send, recv):
+    me = lax.axis_index(axis)
+    peers = [lax.rem(me + i, n) for i in range(1, n)]
+    greet(axis, peers)
+    copies = [
+        sent(axis, peer, x.at[peer], landed.at[i], send.at[i], recv.at[i]) for i, peer in enumerate(peers)
+    ]
+    total = x[me].astype(jnp.float32)
+    for i, copy in enumerate(copies):
+        copy.wait_recv()
+        total = total + landed[i].astype(jnp.float32)
+    out[...] = total
+    for copy in copies:
+        copy.wait_send()
+
+
+def exchanged(x, axis, n, ident):
+    out = jax.ShapeDtypeStruct(x.shape[1:], jnp.float32)
+    scratch = [pltpu.VMEM((n - 1,) + x.shape[1:], x.dtype)]
+    return remote(functools.partial(exchange_kernel, axis, n), out, [x], [n - 1] * 2, scratch, ident, "exchange")
+
+
+def mean_kernel(axis, n, x, out, landed, mine, send, recv, send_out, recv_out):
+    me = lax.axis_index(axis)
+    peers = [lax.rem(me + i, n) for i in range(1, n)]
+    greet(axis, peers)
+    copies = [
+        sent(axis, peer, x.at[peer], landed.at[i], send.at[i], recv.at[i]) for i, peer in enumerate(peers)
+    ]
+    total = x[me]
+    for i, copy in enumerate(copies):
+        copy.wait_recv()
+        total = total + landed[i]
+    mine[...] = total
+    out[me] = total
+    later = [
+        sent(axis, peer, mine, out.at[me], send_out.at[i], recv_out.at[i]) for i, peer in enumerate(peers)
+    ]
+    for copy in copies:
+        copy.wait_send()
+    for copy in later:
+        copy.wait()
+
+
+def summed(x, axis, n, ident):
+    size = x.size // 128
+    if n < 2 or size % (8 * n):
+        return lax.psum(x, axis)
+    parts = x.reshape(n, size // n, 128)
+    scratch = [
+        pltpu.VMEM((n - 1,) + parts.shape[1:], x.dtype),
+        pltpu.VMEM(parts.shape[1:], x.dtype),
+    ]
+    out = jax.ShapeDtypeStruct(parts.shape, x.dtype)
+    kernel = functools.partial(mean_kernel, axis, n)
+    return remote(kernel, out, [parts], [n - 1] * 4, scratch, ident, "mean").reshape(x.shape)
+
+
+def spread_kernel(axis, n, parts, x, out, *sems):
+    me = lax.axis_index(axis)
+    chips = n // 2
+    chip, core = me // 2, lax.rem(me, 2)
+    sibling = me + 1 - 2 * core
+    tiles = x.shape[0] // parts
+    across = [lax.rem(chip + j, chips) * 2 + core for j in range(1, chips)]
+    greet(axis, [sibling] + across)
+    near_send, near_recv, far_send, far_recv, on_send, on_recv = sems
+    copies = []
+    pieces = [pl.ds(p * tiles, tiles) for p in range(parts)]
+    for p, piece in enumerate(pieces):
+        for j, peer in enumerate(across):
+            k = j * parts + p
+            copies.append(sent(axis, peer, x.at[piece], out.at[me, piece], far_send.at[k], far_recv.at[k]))
+    near = sent(axis, sibling, x, out.at[me], near_send.at[0], near_recv.at[0])
+    out[me] = x[...]
+    passed = []
+    for p, piece in enumerate(pieces):
+        for j in range(1, chips):
+            k = (j - 1) * parts + p
+            copies[p * (chips - 1) + j - 1].wait_recv()
+            origin = lax.rem(chip + chips - j, chips) * 2 + core
+            landed = out.at[origin, piece]
+            passed.append(sent(axis, sibling, landed, landed, on_send.at[k], on_recv.at[k]))
+    near.wait()
+    for copy in copies:
+        copy.wait_send()
+    for copy in passed:
+        copy.wait()
+
+
+def spread(x, axis, n, ident):
+    parts = 4 if x.shape[0] % 4 == 0 else 1
+    if n % 2 or n < 4:
+        return gathered(x, axis, n, ident).reshape(-1, *x.shape[1:])
+    out = jax.ShapeDtypeStruct((n,) + x.shape, x.dtype)
+    far = (n // 2 - 1) * parts
+    kernel = functools.partial(spread_kernel, axis, n, parts)
+    return remote(kernel, out, [x], [1, 1, far, far, far, far], [], ident, "spread").reshape(-1, *x.shape[1:])
+
+
+def on_device(areas, scens, wind, load, ptdf_tiles, tile_cols, line_cap, gen_bus, gen_data, prob_weight):
     scen_local, hours, bus_local = wind.shape
     gens = gen_bus.shape[0]
     tile = ptdf_tiles.shape[2]
@@ -204,11 +350,12 @@
     slow = jnp.any(high > low + 1).astype(jnp.int32)[None]
     bus_chunks = bus_local_sorted.reshape(chunks, 1, tile)
 
-    bus_all = lax.all_gather(bus_sorted, "area", axis=0, tiled=True).reshape(-1, 1, tile)
+    bus_all = gathered(bus_sorted.reshape(chunks, tile), "area", areas, 0).reshape(-1, 1, tile)
     group_low = bus_all[:, 0, 0] // tile
     group_high = bus_all[:, 0, -1] // tile
 
-    total = lax.psum(jnp.sum(prob_weight.astype(jnp.float32)), "scen")
+    own = jnp.broadcast_to(jnp.sum(prob_weight.astype(jnp.float32)), (8, 128))
+    total = jnp.sum(gathered(own, "scen", scens, 1)[:, 0, 0])
     probs = jnp.repeat(prob_weight.astype(jnp.float32) / total, hours)[None, :, None]
 
     shape = (chunks, rows, tile)
@@ -226,14 +373,11 @@
         disp_rows = jnp.tile(disp_mean, (1, scen_local, 1))
         for step_index in range(STEPS):
             injection = injected(dispatch, bus_chunks, wind_rows, load_rows, low, high, slow)
-            whole = lax.all_gather(injection, "area", axis=0, tiled=True)
+            whole = spread(injection, "area", areas, 2)
             flow, partial_price, imbalance = flows_and_prices(
                 whole, ptdf_tiles, tile_cols, line_cap, bus_all, group_low, group_high
             )
-            pieces = lax.all_to_all(
-                partial_price.reshape(areas, chunks, rows, tile), "area", 0, 0
-            )
-            price_gen = jnp.sum(pieces.astype(jnp.float32), axis=0)
+            price_gen = exchanged(partial_price.reshape(areas, chunks, rows, tile), "area", areas, 3)
             grad = (
                 linear
                 + quadratic * dispatch
@@ -252,7 +396,7 @@
             dispatch = jnp.clip(dispatch - step_gen * grad, 0.0, capacity * commit)
         both = jnp.stack([probs * commit, probs * dispatch])
         both = jnp.sum(both.reshape(2, chunks, scen_local, hours, tile), axis=2)
-        comm_mean, disp_mean = lax.psum(both, "scen")
+        comm_mean, disp_mean = summed(both, "scen", scens, 4)
         w_comm = w_comm + penalty * (commit - jnp.tile(comm_mean, (1, scen_local, 1)))
         w_disp = w_disp + penalty * (dispatch - jnp.tile(disp_mean, (1, scen_local, 1)))
 
@@ -281,7 +425,7 @@
         P("scen"),
     )
     return jax.shard_map(
-        functools.partial(on_device, mesh.shape["area"]),
+        functools.partial(on_device, mesh.shape["area"], mesh.shape["scen"]),
         mesh=mesh,
         in_specs=placed,
         out_specs=(

time: 381 us -> 291 us (0.76)
  waiting for transfers between devices: 165 us -> 0 us
  Pallas kernels: 130 us -> 251 us
  blocking collectives: 28.1 us -> 0 us
  starting transfers between devices: 13.7 us -> 0 us
  between operations: 16.2 us -> 2.87 us
  local copies, waits for them, and re-layouts: 10.2 us -> 16 us
    pallas_call x0 -> x12, Pallas kernels: none -> 121 us  [remote(): pl.pallas_call(kernel, in_specs=[VMEM] * len(args), out_specs=VMEM, out_s...]
    psum x2 -> x0, waiting for transfers between devices: 98.9 us -> none  [on_device(): comm_mean, disp_mean = lax.psum(both, 'scen')]
    all_gather x4 -> x0, waiting for transfers between devices: 45.1 us -> none  [on_device(): whole = lax.all_gather(injection, 'area', axis=0, tiled=True)]
    psum x1 -> x0, blocking collectives: 21.9 us -> none  [on_device(): total = lax.psum(jnp.sum(prob_weight.astype(jnp.float32)), 'scen')]
    all_to_all x4 -> x0, waiting for transfers between devices: 20.8 us -> none  [on_device(): lax.all_to_all(partial_price.reshape(areas, chunks, rows, tile), 'area',...]
    all_to_all x4 -> x0, starting transfers between devices: 13.5 us -> none  [on_device(): lax.all_to_all(partial_price.reshape(areas, chunks, rows, tile), 'area',...]
    all_gather x1 -> x0, blocking collectives: 6.22 us -> none  [on_device(): lax.all_gather(bus_sorted, 'area', axis=0, tiled=True).reshape(-1, 1, tile)]
    another operation x2 -> x6, other arithmetic: 1.38 us -> 7.23 us  [on_device(): both = jnp.stack([probs * commit, probs * dispatch])]
  transfers between devices with their start and end apart: 10 -> 0, of which waited for: 9 -> 0; matrix products, arithmetic and copies ran while one was open for 1% -> 0% of each run, Pallas kernels for 8% -> 0%
where the time goes in v2:
time: 291 us; the launch traced here: 288 us
  Pallas kernels  251 us (86%)
  local copies, waits for them, and re-layouts  16 us (5%)
  other arithmetic  13.7 us (5%)
  matrix products  4.47 us (2%)
    pallas_call x12, Pallas kernels, remote(): pl.pallas_call(kernel, in_specs=[VMEM] * len(args), out_specs=VMEM, out_s...  121 us
    pallas_call x4, Pallas kernels, flows_and_prices(): pl.pallas_call(flow_kernel, grid_spec=pltpu.PrefetchScalarGridSpec(num_sc...  117 us
    pallas_call x4, Pallas kernels, injected(): pl.pallas_call(inject_kernel, in_specs=[smem] * 3 + [vmem] * 4, out_specs...  12.4 us
    unnamed x30, local copies, waits for them, and re-layouts  9.22 us
    another operation x6, other arithmetic, on_device(): both = jnp.stack([probs * commit, probs * dispatch])  7.23 us

profile of v2, /device:TPU:0, one launch (start us, length us, event | category | flops | bytes accessed | tf_op | source)
XLA Modules:
  0.0 287.9 jit_solution(8220253974580188915)
XLA Ops:
  1.3 0.8 reshape.154.cols_sm
  2.1 1.6 convert_reduce_fusion
  3.7 0.7 convert_element_type.32
  5.0 2.2 fusion.1
  8.6 1.3 compare_reduce_fusion
  10.5 5.9 %gather.3 = s32[4,8,128]{2,1,0:T(8,128)} custom-call(s32[8,128]{1,0:T(8,128)} %bitcast.95), custom_call_target="tpu_custom_call" | custom-call | tf_op jit(solution)/shard_map/gather/pallas_call | solution.py:195
  16.4 2.1 slice_reduce_fusion
  18.5 8.8 %gather.2 = f32[8,8,128]{2,1,0:T(8,128)} custom-call(f32[8,128]{1,0:T(8,128)} %broadcast_in_dim.8.x), custom_call_target="tpu_custom_call" | custom-call | tf_op jit(solution)/shard_map/gather/pallas_call | solution.py:195
  27.4 1.4 slice_reduce_fusion.2
  29.4 0.6 add.142.disp
  30.1 3.1 %inject.4.x = bf16[48,24,128]{2,1,0:T(8,128)(2,1)} custom-call(s32[48]{0:T(128)} %get-tuple-element.38.lo_sm, s32[48]{0:T(128)} %get-tuple-element.37.hi_sm, s32[1]{0:T(128)} %bitcast.11.slow_sm, f32[8,24,128]{2,1,0:T(8,128)} %add.142.disp, s32[8,1,128]{2,1,0:T(1,128)} %fusion.29.bus, bf16[24,6144]{1,0:T(8,128)(2,1)} %bitcast.66, bf16[24,6144]{1,0:T(8,128)(2,1)} %load.7), custom_call_target="tpu_custom_call" | custom-call | tf_op jit(solution)/shard_map/inject/pallas_call | solution.py:165
  33.2 12.2 %spread.4 = bf16[4,48,24,128]{3,2,1,0:T(8,128)(2,1)} custom-call(bf16[48,24,128]{2,1,0:T(8,128)(2,1)} %inject.4.x), custom_call_target="tpu_custom_call" | custom-call | tf_op jit(solution)/shard_map/spread/pallas_call | solution.py:195
  45.4 1.3 copy-done.1
  46.7 0.7 copy-done.4
  47.4 0.7 copy-done.6
  48.1 29.3 %flow_step.4 = (f32[24,4096]{1,0:T(8,128)}, bf16[32,24,128]{2,1,0:T(8,128)(2,1)S(1)}, f32[24,128]{1,0:T(8,128)S(1)}) custom-call(s32[1024]{0:T(1024)S(1)} %reshape.154.cols_sm, s32[32]{0:T(128)S(1)} %get-tuple-element.57.lo_sm, s32[32]{0:T(128)S(1)} %get-tuple-element.56.hi_sm, bf16[192,24,128]{2,1,0:T(8,128)(2,1)S(1)} %bitcast.50, ...), custom_call_target="tpu_custom_call" | custom-call | tf_op jit(solution)/shard_map/flow_step/pallas_call | solution.py:88
  77.4 0.7 copy-done.9
  78.1 6.2 %exchange.4 = f32[8,24,128]{2,1,0:T(8,128)} custom-call(bf16[4,8,24,128]{3,2,1,0:T(8,128)(2,1)} %bitcast.63), custom_call_target="tpu_custom_call" | custom-call | tf_op jit(solution)/shard_map/exchange/pallas_call | solution.py:195
  84.3 1.6 multiply_bitcast_fusion.3
  85.9 3.1 %inject.5.x = bf16[48,24,128]{2,1,0:T(8,128)(2,1)} custom-call(s32[48]{0:T(128)} %get-tuple-element.38.lo_sm, s32[48]{0:T(128)} %get-tuple-element.37.hi_sm, s32[1]{0:T(128)} %bitcast.11.slow_sm, f32[8,24,128]{2,1,0:T(8,128)} %get-tuple-element.31.disp, s32[8,1,128]{2,1,0:T(1,128)} %fusion.29.bus, bf16[24,6144]{1,0:T(8,128)(2,1)} %bitcast.67, ...), custom_call_target="tpu_custom_call" | custom-call | tf_op jit(solution)/shard_map/inject/pallas_call | solution.py:165
  88.9 12.3 %spread.5 = bf16[4,48,24,128]{3,2,1,0:T(8,128)(2,1)} custom-call(bf16[48,24,128]{2,1,0:T(8,128)(2,1)} %inject.5.x), custom_call_target="tpu_custom_call" | custom-call | tf_op jit(solution)/shard_map/spread/pallas_call | solution.py:195
  101.3 1.3 copy-done.2
  102.6 29.3 %flow_step.5 = (f32[24,4096]{1,0:T(8,128)}, bf16[32,24,128]{2,1,0:T(8,128)(2,1)S(1)}, f32[24,128]{1,0:T(8,128)S(1)}) custom-call(s32[1024]{0:T(1024)S(1)} %reshape.154.cols_sm, s32[32]{0:T(128)S(1)} %get-tuple-element.57.lo_sm, s32[32]{0:T(128)S(1)} %get-tuple-element.56.hi_sm, bf16[192,24,128]{2,1,0:T(8,128)(2,1)S(1)} %bitcast.51, ...), custom_call_target="tpu_custom_call" | custom-call | tf_op jit(solution)/shard_map/flow_step/pallas_call | solution.py:88
  131.8 0.7 copy-done.10
  132.5 6.2 %exchange.5 = f32[8,24,128]{2,1,0:T(8,128)} custom-call(bf16[4,8,24,128]{3,2,1,0:T(8,128)(2,1)} %bitcast.64), custom_call_target="tpu_custom_call" | custom-call | tf_op jit(solution)/shard_map/exchange/pallas_call | solution.py:195
  138.7 1.6 multiply_bitcast_fusion.2
  140.3 0.7 pad_maximum_fusion
  141.0 17.0 %mean.2 = f32[8,48,128]{2,1,0:T(8,128)} custom-call(f32[8,48,128]{2,1,0:T(8,128)} %bitcast.72), custom_call_target="tpu_custom_call" | custom-call | tf_op jit(solution)/shard_map/mean/pallas_call | solution.py:195
  158.1 1.0 fusion.26
  159.0 3.1 %inject.6.x = bf16[48,24,128]{2,1,0:T(8,128)(2,1)} custom-call(s32[48]{0:T(128)} %get-tuple-element.38.lo_sm, s32[48]{0:T(128)} %get-tuple-element.37.hi_sm, s32[1]{0:T(128)} %bitcast.11.slow_sm, f32[8,24,128]{2,1,0:T(8,128)} %get-tuple-element.33.disp, s32[8,1,128]{2,1,0:T(1,128)} %fusion.29.bus, bf16[24,6144]{1,0:T(8,128)(2,1)} %bitcast.68, ...), custom_call_target="tpu_custom_call" | custom-call | tf_op jit(solution)/shard_map/inject/pallas_call | solution.py:165
  162.1 11.3 %spread.6 = bf16[4,48,24,128]{3,2,1,0:T(8,128)(2,1)} custom-call(bf16[48,24,128]{2,1,0:T(8,128)(2,1)} %inject.6.x), custom_call_target="tpu_custom_call" | custom-call | tf_op jit(solution)/shard_map/spread/pallas_call | solution.py:195
  173.4 1.3 copy-done.3
  174.7 29.3 %flow_step.6 = (f32[24,4096]{1,0:T(8,128)}, bf16[32,24,128]{2,1,0:T(8,128)(2,1)S(1)}, f32[24,128]{1,0:T(8,128)S(1)}) custom-call(s32[1024]{0:T(1024)S(1)} %reshape.154.cols_sm, s32[32]{0:T(128)S(1)} %get-tuple-element.57.lo_sm, s32[32]{0:T(128)S(1)} %get-tuple-element.56.hi_sm, bf16[192,24,128]{2,1,0:T(8,128)(2,1)S(1)} %bitcast.52, ...), custom_call_target="tpu_custom_call" | custom-call | tf_op jit(solution)/shard_map/flow_step/pallas_call | solution.py:88
  203.9 0.7 copy-done.11
  204.6 6.2 %exchange.6 = f32[8,24,128]{2,1,0:T(8,128)} custom-call(bf16[4,8,24,128]{3,2,1,0:T(8,128)(2,1)} %bitcast.65), custom_call_target="tpu_custom_call" | custom-call | tf_op jit(solution)/shard_map/exchange/pallas_call | solution.py:195
  210.8 1.7 multiply_bitcast_fusion.1
  212.5 3.2 %inject.7.x = bf16[48,24,128]{2,1,0:T(8,128)(2,1)} custom-call(s32[48]{0:T(128)} %get-tuple-element.38.lo_sm, s32[48]{0:T(128)} %get-tuple-element.37.hi_sm, s32[1]{0:T(128)} %bitcast.11.slow_sm, f32[8,24,128]{2,1,0:T(8,128)} %get-tuple-element.26.disp, s32[8,1,128]{2,1,0:T(1,128)} %fusion.29.bus, bf16[24,6144]{1,0:T(8,128)(2,1)} %bitcast.69, ...), custom_call_target="tpu_custom_call" | custom-call | tf_op jit(solution)/shard_map/inject/pallas_call | solution.py:165
  215.7 12.3 %spread.7 = bf16[4,48,24,128]{3,2,1,0:T(8,128)(2,1)} custom-call(bf16[48,24,128]{2,1,0:T(8,128)(2,1)} %inject.7.x), custom_call_target="tpu_custom_call" | custom-call | tf_op jit(solution)/shard_map/spread/pallas_call | solution.py:195
  228.1 1.3 copy-done
  229.4 29.3 %flow_step.7 = (f32[24,4096]{1,0:T(8,128)}, bf16[32,24,128]{2,1,0:T(8,128)(2,1)S(1)}, f32[24,128]{1,0:T(8,128)S(1)}) custom-call(s32[1024]{0:T(1024)S(1)} %reshape.154.cols_sm, s32[32]{0:T(128)S(1)} %get-tuple-element.57.lo_sm, s32[32]{0:T(128)S(1)} %get-tuple-element.56.hi_sm, bf16[192,24,128]{2,1,0:T(8,128)(2,1)S(1)} %bitcast.49, ...), custom_call_target="tpu_custom_call" | custom-call | tf_op jit(solution)/shard_map/flow_step/pallas_call | solution.py:88
  258.6 0.7 copy-done.8
  259.3 6.2 %exchange.7 = f32[8,24,128]{2,1,0:T(8,128)} custom-call(bf16[4,8,24,128]{3,2,1,0:T(8,128)(2,1)} %bitcast.62), custom_call_target="tpu_custom_call" | custom-call | tf_op jit(solution)/shard_map/exchange/pallas_call | solution.py:195
  265.5 1.0 multiply_bitcast_fusion
  266.5 0.7 pad_maximum_fusion.1
  267.2 16.7 %mean.3 = f32[8,48,128]{2,1,0:T(8,128)} custom-call(f32[8,48,128]{2,1,0:T(8,128)} %bitcast.73), custom_call_target="tpu_custom_call" | custom-call | tf_op jit(solution)/shard_map/mean/pallas_call | solution.py:195
  283.9 1.0 fusion.25
  284.9 2.3 fusion
  287.2 0.7 slice_bitcast_fusion
  (33 shorter events, 2.1 us)
Async XLA Ops:
  45.4 1.3 copy-start.1
  46.7 0.7 copy-start.4
  47.4 0.7 copy-start.6
  48.1 53.2 %copy-start.5 = (s32[4,8,128]{2,1,0:T(8,128)S(1)}, s32[4,8,128]{2,1,0:T(8,128)}, u32[]{:S(2)}) copy-start(s32[4,8,128]{2,1,0:T(8,128)} %gather.3) | copy-start | bytes 49156
  48.1 53.2 %copy-start.7 = (f32[4096]{0:T(1024)S(1)}, f32[4096]{0:T(1024)}, u32[]{:S(2)}) copy-start(f32[4096]{0:T(1024)} %param.12) | copy-start | bytes 49156
  77.4 0.7 copy-start.9
  101.3 1.3 copy-start.2
  102.6 36.2 %copy-start.12 = (f32[8,24,128]{2,1,0:T(8,128)S(1)}, f32[8,24,128]{2,1,0:T(8,128)}, u32[]{:S(2)}) copy-start(f32[8,24,128]{2,1,0:T(8,128)} %get-tuple-element.31.disp) | copy-start | bytes 294916
  131.8 0.7 copy-start.10
  173.4 1.3 copy-start.3
  174.7 36.2 %copy-start.14 = (f32[8,24,128]{2,1,0:T(8,128)S(1)}, f32[8,24,128]{2,1,0:T(8,128)}, u32[]{:S(2)}) copy-start(f32[8,24,128]{2,1,0:T(8,128)} %get-tuple-element.33.disp) | copy-start | bytes 294916
  203.9 0.7 copy-start.11
  228.1 1.3 copy-start
  229.4 36.2 %copy-start.13 = (f32[8,24,128]{2,1,0:T(8,128)S(1)}, f32[8,24,128]{2,1,0:T(8,128)}, u32[]{:S(2)}) copy-start(f32[8,24,128]{2,1,0:T(8,128)} %get-tuple-element.26.disp) | copy-start | bytes 294916
  258.6 0.7 copy-start.8

commit v3 on v1

--- a/solution.py
+++ b/solution.py
@@ -42,7 +42,7 @@
         own = [cols_sm[base + z] for z in range(slots)]
         picked = jnp.concatenate([inj[c] for c in own], axis=1)
         wide = jnp.concatenate([w[kk, z] for z in range(slots)], axis=1)
-        flows.append(lax.dot_general(picked, wide, NT, preferred_element_type=jnp.float32))
+        flows.append(lax.dot_general(wide, picked, NT, preferred_element_type=jnp.float32).T)
         cols.append(own)
     contribs = []
     for kk in range(block):
@@ -80,7 +80,7 @@
         lax.fori_loop(0, bus.shape[0], one, 0)
 
 
-def flows_and_prices(inj, w, cols, cap, bus, low, high, block=2):
+def flows_and_prices(inj, w, cols, cap, bus, low, high, block=4):
     tiles, rows, tile = inj.shape
     lines, slots = w.shape[0], w.shape[1]
     block = block if lines % block == 0 else 1
@@ -172,7 +172,244 @@
     )(low, high, slow, disp, bus, wind, load)
 
 
-def on_device(areas, wind, load, ptdf_tiles, tile_cols, line_cap, gen_bus, gen_data, prob_weight):
+MESH = pl.DeviceIdType.MESH
+VMEM = pl.BlockSpec(memory_space=pltpu.VMEM)
+
+
+def greet(axis, peers):
+    barrier = pltpu.get_barrier_semaphore()
+    for peer in peers:
+        pl.semaphore_signal(barrier, inc=1, device_id={axis: peer}, device_id_type=MESH)
+    pl.semaphore_wait(barrier, len(peers))
+
+
+def sent(axis, peer, src, dst, send, recv):
+    copy = pltpu.make_async_remote_copy(
+        src_ref=src, dst_ref=dst, send_sem=send, recv_sem=recv, device_id={axis: peer}, device_id_type=MESH
+    )
+    copy.start()
+    return copy
+
+
+def remote(kernel, out, args, sems, scratch, ident, name):
+    return pl.pallas_call(
+        kernel,
+        in_specs=[VMEM] * len(args),
+        out_specs=VMEM,
+        out_shape=out,
+        scratch_shapes=list(scratch) + [pltpu.SemaphoreType.DMA((k,)) for k in sems],
+        compiler_params=pltpu.CompilerParams(collective_id=ident, has_side_effects=True),
+        name=name,
+    )(*args)
+
+
+def gather_kernel(axis, n, x, out, send, recv):
+    me = lax.axis_index(axis)
+    peers = [lax.rem(me + i, n) for i in range(1, n)]
+    greet(axis, peers)
+    copies = [sent(axis, peer, x, out.at[me], send.at[i], recv.at[i]) for i, peer in enumerate(peers)]
+    out[me] = x[...]
+    for copy in copies:
+        copy.wait()
+
+
+def gathered(x, axis, n, ident):
+    out = jax.ShapeDtypeStruct((n,) + x.shape, x.dtype)
+    return remote(functools.partial(gather_kernel, axis, n), out, [x], [n - 1] * 2, [], ident, "gather")
+
+
+def exchange_kernel(axis, n, x, out, landed, send, recv):
+    me = lax.axis_index(axis)
+    peers = [lax.rem(me + i, n) for i in range(1, n)]
+    greet(axis, peers)
+    copies = [
+        sent(axis, peer, x.at[peer], landed.at[i], send.at[i], recv.at[i]) for i, peer in enumerate(peers)
+    ]
+    total = x[me].astype(jnp.float32)
+    for i, copy in enumerate(copies):
+        copy.wait_recv()
+        total = total + landed[i].astype(jnp.float32)
+    out[...] = total
+    for copy in copies:
+        copy.wait_send()
+
+
+def exchanged(x, axis, n, ident):
+    out = jax.ShapeDtypeStruct(x.shape[1:], jnp.float32)
+    scratch = [pltpu.VMEM((n - 1,) + x.shape[1:], x.dtype)]
+    return remote(functools.partial(exchange_kernel, axis, n), out, [x], [n - 1] * 2, scratch, ident, "exchange")
+
+
+class Mean:
+    def __init__(self, axis, n, x, out, landed, mine, send, recv, send_out, recv_out):
+        self.me = lax.axis_index(axis)
+        self.axis, self.x, self.out, self.landed, self.mine = axis, x, out, landed, mine
+        self.sems = send, recv, send_out, recv_out
+        self.peers = [lax.rem(self.me + i, n) for i in range(1, n)]
+        self.greeted = axis, self.peers
+
+    def start(self):
+        send, recv = self.sems[:2]
+        self.copies = [
+            sent(self.axis, peer, self.x.at[peer], self.landed.at[i], send.at[i], recv.at[i])
+            for i, peer in enumerate(self.peers)
+        ]
+
+    def middle(self):
+        send, recv = self.sems[2:]
+        total = self.x[self.me]
+        for i, copy in enumerate(self.copies):
+            copy.wait_recv()
+            total = total + self.landed[i]
+        self.mine[...] = total
+        self.out[self.me] = total
+        self.later = [
+            sent(self.axis, peer, self.mine, self.out.at[self.me], send.at[i], recv.at[i])
+            for i, peer in enumerate(self.peers)
+        ]
+
+    def finish(self):
+        for copy in self.copies:
+            copy.wait_send()
+        for copy in self.later:
+            copy.wait()
+
+
+class Spread:
+    def __init__(self, axis, n, parts, x, out, *sems):
+        self.me = lax.axis_index(axis)
+        self.axis, self.parts, self.x, self.out, self.sems = axis, parts, x, out, sems
+        self.chips = n // 2
+        self.chip, self.core = self.me // 2, lax.rem(self.me, 2)
+        self.sibling = self.me + 1 - 2 * self.core
+        self.across = [lax.rem(self.chip + j, self.chips) * 2 + self.core for j in range(1, self.chips)]
+        self.greeted = axis, [self.sibling] + self.across
+        tiles = x.shape[0] // parts
+        self.pieces = [pl.ds(p * tiles, tiles) for p in range(parts)]
+
+    def start(self):
+        near_send, near_recv, far_send, far_recv = self.sems[:4]
+        me, x, out = self.me, self.x, self.out
+        self.copies = []
+        for p, piece in enumerate(self.pieces):
+            for j, peer in enumerate(self.across):
+                k = j * self.parts + p
+                self.copies.append(
+                    sent(self.axis, peer, x.at[piece], out.at[me, piece], far_send.at[k], far_recv.at[k])
+                )
+        self.near = sent(self.axis, self.sibling, x, out.at[me], near_send.at[0], near_recv.at[0])
+        out[me] = x[...]
+
+    def middle(self):
+        on_send, on_recv = self.sems[4:]
+        chips = self.chips
+        self.passed = []
+        for p, piece in enumerate(self.pieces):
+            for j in range(1, chips):
+                k = (j - 1) * self.parts + p
+                self.copies[p * (chips - 1) + j - 1].wait_recv()
+                origin = lax.rem(self.chip + chips - j, chips) * 2 + self.core
+                landed = self.out.at[origin, piece]
+                self.passed.append(
+                    sent(self.axis, self.sibling, landed, landed, on_send.at[k], on_recv.at[k])
+                )
+
+    def finish(self):
+        self.near.wait()
+        for copy in self.copies:
+            copy.wait_send()
+        for copy in self.passed:
+            copy.wait()
+
+
+def greet_all(groups):
+    barrier = pltpu.get_barrier_semaphore()
+    for axis, peers in groups:
+        for peer in peers:
+            pl.semaphore_signal(barrier, inc=1, device_id={axis: peer}, device_id_type=MESH)
+    pl.semaphore_wait(barrier, sum(len(peers) for _, peers in groups))
+
+
+def transfers_kernel(moves, *refs):
+    count = len(moves)
+    sources, outs, rest = refs[:count], refs[count:2 * count], refs[2 * count:]
+    runs = []
+    for (make, own, _, _, _), x, out in zip(moves, sources, outs):
+        runs.append(make(x, out, *rest[:own]))
+        rest = rest[own:]
+    greet_all([run.greeted for run in runs])
+    for phase in ("start", "middle", "finish"):
+        for run in runs:
+            getattr(run, phase)()
+
+
+def transferred(moves, ident, name):
+    args = [move[2] for move in moves]
+    return pl.pallas_call(
+        functools.partial(transfers_kernel, [move[:2] + (None,) * 3 for move in moves]),
+        in_specs=[VMEM] * len(args),
+        out_specs=[VMEM] * len(args),
+        out_shape=[move[3] for move in moves],
+        scratch_shapes=[entry for move in moves for entry in move[4]],
+        compiler_params=pltpu.CompilerParams(collective_id=ident, has_side_effects=True),
+        name=name,
+    )(*args)
+
+
+def dma(*counts):
+    return [pltpu.SemaphoreType.DMA((k,)) for k in counts]
+
+
+def mean_move(x, axis, n):
+    scratch = [pltpu.VMEM((n - 1,) + x.shape[1:], x.dtype), pltpu.VMEM(x.shape[1:], x.dtype)]
+    scratch += dma(n - 1, n - 1, n - 1, n - 1)
+    return functools.partial(Mean, axis, n), len(scratch), x, jax.ShapeDtypeStruct(x.shape, x.dtype), scratch
+
+
+def spread_move(x, axis, n):
+    parts = 4 if x.shape[0] % 4 == 0 else 1
+    far = (n // 2 - 1) * parts
+    scratch = dma(1, 1, far, far, far, far)
+    out = jax.ShapeDtypeStruct((n,) + x.shape, x.dtype)
+    return functools.partial(Spread, axis, n, parts), len(scratch), x, out, scratch
+
+
+def in_parts(both, weight, n):
+    size = both.size // 128
+    if n < 2 or size % (8 * n):
+        return None
+    parts = both.reshape(n, size // n, 128)
+    return jnp.concatenate([parts, jnp.broadcast_to(weight, (n, 8, 128))], axis=1)
+
+
+def from_parts(parts, shape):
+    return (parts[:, :-8] / parts[:, -8:-7]).reshape(shape)
+
+
+def averaged(both, weight, axis, n, ident):
+    parts = in_parts(both, weight, n)
+    if parts is None:
+        return lax.psum(both, axis) / lax.psum(weight, axis)
+    (out,) = transferred([mean_move(parts, axis, n)], ident, "mean")
+    return from_parts(out, both.shape)
+
+
+def spread(x, axis, n, ident):
+    if n % 2 or n < 4:
+        return gathered(x, axis, n, ident).reshape(-1, *x.shape[1:])
+    (out,) = transferred([spread_move(x, axis, n)], ident, "spread")
+    return out.reshape(-1, *x.shape[1:])
+
+
+def spread_and_averaged(x, axis, n, both, weight, other, m, idents):
+    parts = in_parts(both, weight, m)
+    if parts is None or n % 2 or n < 4:
+        return spread(x, axis, n, idents[0]), averaged(both, weight, other, m, idents[1])
+    mean, out = transferred([mean_move(parts, other, m), spread_move(x, axis, n)], idents[2], "spread_mean")
+    return out.reshape(-1, *x.shape[1:]), from_parts(mean, both.shape)
+
+
+def on_device(areas, scens, wind, load, ptdf_tiles, tile_cols, line_cap, gen_bus, gen_data, prob_weight):
     scen_local, hours, bus_local = wind.shape
     gens = gen_bus.shape[0]
     tile = ptdf_tiles.shape[2]
@@ -204,12 +441,13 @@
     slow = jnp.any(high > low + 1).astype(jnp.int32)[None]
     bus_chunks = bus_local_sorted.reshape(chunks, 1, tile)
 
-    bus_all = lax.all_gather(bus_sorted, "area", axis=0, tiled=True).reshape(-1, 1, tile)
+    bus_all = gathered(bus_sorted.reshape(chunks, tile), "area", areas, 0).reshape(-1, 1, tile)
     group_low = bus_all[:, 0, 0] // tile
     group_high = bus_all[:, 0, -1] // tile
 
-    total = lax.psum(jnp.sum(prob_weight.astype(jnp.float32)), "scen")
-    probs = jnp.repeat(prob_weight.astype(jnp.float32) / total, hours)[None, :, None]
+    weight = prob_weight.astype(jnp.float32)
+    weights = jnp.repeat(weight, hours)[None, :, None]
+    weight = jnp.sum(weight)
 
     shape = (chunks, rows, tile)
     commit = jnp.full(shape, 0.5, jnp.float32)
@@ -221,19 +459,26 @@
     wind_rows = wind.reshape(rows, bus_local)
     load_rows = jnp.tile(load, (scen_local, 1))
     flow = None
+    both = None
     for round_index in range(ITERS):
-        comm_rows = jnp.tile(comm_mean, (1, scen_local, 1))
-        disp_rows = jnp.tile(disp_mean, (1, scen_local, 1))
         for step_index in range(STEPS):
             injection = injected(dispatch, bus_chunks, wind_rows, load_rows, low, high, slow)
-            whole = lax.all_gather(injection, "area", axis=0, tiled=True)
+            if both is None:
+                whole = spread(injection, "area", areas, 2)
+            else:
+                whole, means = spread_and_averaged(
+                    injection, "area", areas, both, weight, "scen", scens, (2, 4, 5)
+                )
+                comm_mean, disp_mean = means
+                w_comm = w_comm + penalty * (commit - jnp.tile(comm_mean, (1, scen_local, 1)))
+                w_disp = w_disp + penalty * (dispatch - jnp.tile(disp_mean, (1, scen_local, 1)))
+                both = None
+            comm_rows = jnp.tile(comm_mean, (1, scen_local, 1))
+            disp_rows = jnp.tile(disp_mean, (1, scen_local, 1))
             flow, partial_price, imbalance = flows_and_prices(
                 whole, ptdf_tiles, tile_cols, line_cap, bus_all, group_low, group_high
             )
-            pieces = lax.all_to_all(
-                partial_price.reshape(areas, chunks, rows, tile), "area", 0, 0
-            )
-            price_gen = jnp.sum(pieces.astype(jnp.float32), axis=0)
+            price_gen = exchanged(partial_price.reshape(areas, chunks, rows, tile), "area", areas, 3)
             grad = (
                 linear
                 + quadratic * dispatch
@@ -250,11 +495,9 @@
                 1.0,
             )
             dispatch = jnp.clip(dispatch - step_gen * grad, 0.0, capacity * commit)
-        both = jnp.stack([probs * commit, probs * dispatch])
+        both = jnp.stack([weights * commit, weights * dispatch])
         both = jnp.sum(both.reshape(2, chunks, scen_local, hours, tile), axis=2)
-        comm_mean, disp_mean = lax.psum(both, "scen")
-        w_comm = w_comm + penalty * (commit - jnp.tile(comm_mean, (1, scen_local, 1)))
-        w_disp = w_disp + penalty * (dispatch - jnp.tile(disp_mean, (1, scen_local, 1)))
+    comm_mean, disp_mean = averaged(both, weight, "scen", scens, 4)
 
     outs = jnp.concatenate([comm_mean, disp_mean, dispatch], axis=1)
     outs = jnp.moveaxis(outs, 0, 1).reshape(-1, gens)
@@ -281,7 +524,7 @@
         P("scen"),
     )
     return jax.shard_map(
-        functools.partial(on_device, mesh.shape["area"]),
+        functools.partial(on_device, mesh.shape["area"], mesh.shape["scen"]),
         mesh=mesh,
         in_specs=placed,
         out_specs=(

time: 381 us -> 247 us (0.65)
  waiting for transfers between devices: 165 us -> 0 us
  Pallas kernels: 130 us -> 211 us
  blocking collectives: 28.1 us -> 0 us
  between operations: 16.2 us -> 2.22 us
  starting transfers between devices: 13.7 us -> 0 us
  local copies, waits for them, and re-layouts: 10.2 us -> 15.6 us
    pallas_call x0 -> x10, Pallas kernels: none -> 105 us  [the longest x5 74.3 us: transferred(): pl.pallas_call(functools.partial(transfers_kernel, [move[:2] + (None,) *...]
    psum x2 -> x0, waiting for transfers between devices: 98.9 us -> none  [on_device(): comm_mean, disp_mean = lax.psum(both, 'scen')]
    all_gather x4 -> x0, waiting for transfers between devices: 45.1 us -> none  [on_device(): whole = lax.all_gather(injection, 'area', axis=0, tiled=True)]
    pallas_call x4, Pallas kernels: 117 us -> 93.3 us  [flows_and_prices(): pl.pallas_call(flow_kernel, grid_spec=pltpu.PrefetchScalarGridSpec(num_sc...]
    psum x1 -> x0, blocking collectives: 21.9 us -> none  [on_device(): total = lax.psum(jnp.sum(prob_weight.astype(jnp.float32)), 'scen')]
    all_to_all x4 -> x0, waiting for transfers between devices: 20.8 us -> none  [on_device(): lax.all_to_all(partial_price.reshape(areas, chunks, rows, tile), 'area',...]
    all_to_all x4 -> x0, starting transfers between devices: 13.5 us -> none  [on_device(): lax.all_to_all(partial_price.reshape(areas, chunks, rows, tile), 'area',...]
    all_gather x1 -> x0, blocking collectives: 6.22 us -> none  [on_device(): lax.all_gather(bus_sorted, 'area', axis=0, tiled=True).reshape(-1, 1, tile)]
  transfers between devices with their start and end apart: 10 -> 0, of which waited for: 9 -> 0; matrix products, arithmetic and copies ran while one was open for 1% -> 0% of each run, Pallas kernels for 8% -> 0%
where the time goes in v3:
time: 247 us; the launch traced here: 245 us
  Pallas kernels  211 us (85%)
  local copies, waits for them, and re-layouts  15.6 us (6%)
  other arithmetic  11.9 us (5%)
  matrix products  4.47 us (2%)
    pallas_call x4, Pallas kernels, flows_and_prices(): pl.pallas_call(flow_kernel, grid_spec=pltpu.PrefetchScalarGridSpec(num_sc...  93.3 us
    pallas_call x5, Pallas kernels, transferred(): pl.pallas_call(functools.partial(transfers_kernel, [move[:2] + (None,) *...  74.3 us
    pallas_call x5, Pallas kernels, remote(): pl.pallas_call(kernel, in_specs=[VMEM] * len(args), out_specs=VMEM, out_s...  30.7 us
    pallas_call x4, Pallas kernels, injected(): pl.pallas_call(inject_kernel, in_specs=[smem] * 3 + [vmem] * 4, out_specs...  12.4 us
    unnamed x32, local copies, waits for them, and re-layouts  9.21 us
    another operation x6, other arithmetic, on_device(): both = jnp.stack([weights * commit, weights * dispatch])  5.87 us

profile of v3, /device:TPU:0, one launch (start us, length us, event | category | flops | bytes accessed | tf_op | source)
XLA Modules:
  0.0 244.9 jit_solution(174181666937081014)
XLA Ops:
  1.3 0.8 reshape.154.cols_sm
  2.1 1.6 convert_reduce_fusion
  3.7 0.7 convert_element_type.34
  4.4 2.2 fusion.1
  6.6 0.6 fusion.29.bus
  7.2 0.6 fusion.27
  7.8 0.2 convert_reduce_fusion.1
  8.0 1.3 compare_reduce_fusion
  9.9 5.9 %gather.1 = s32[4,8,128]{2,1,0:T(8,128)} custom-call(s32[8,128]{1,0:T(8,128)} %bitcast.97), custom_call_target="tpu_custom_call" | custom-call | tf_op jit(solution)/shard_map/gather/pallas_call | solution.py:195
  15.8 2.1 slice_reduce_fusion
  17.9 0.6 add.146.disp
  18.6 3.1 %inject.4.refs_0_ = bf16[48,24,128]{2,1,0:T(8,128)(2,1)} custom-call(s32[48]{0:T(128)} %get-tuple-element.42.lo_sm, s32[48]{0:T(128)} %get-tuple-element.41.hi_sm, s32[1]{0:T(128)} %bitcast.9.slow_sm, f32[8,24,128]{2,1,0:T(8,128)} %add.146.disp, s32[8,1,128]{2,1,0:T(1,128)} %fusion.29.bus, bf16[24,6144]{1,0:T(8,128)(2,1)} %bitcast.66, bf16[24,6144]{1,0:T(8,128)(2,1)} %load.7), custom_call_target="tpu_custom_call" | custom-call | tf_op jit(solution)/shard_map/inject/pallas_call | solution.py:165
  21.6 12.8 %spread.3 = bf16[4,48,24,128]{3,2,1,0:T(8,128)(2,1)} custom-call(bf16[48,24,128]{2,1,0:T(8,128)(2,1)} %inject.4.refs_0_), custom_call_target="tpu_custom_call" | custom-call | tf_op jit(solution)/shard_map/spread/pallas_call | solution.py:348
  34.4 1.3 copy-done.1
  35.7 0.7 copy-done.4
  36.4 0.7 copy-done.6
  37.1 23.3 %flow_step.4 = (f32[24,4096]{1,0:T(8,128)}, bf16[32,24,128]{2,1,0:T(8,128)(2,1)S(1)}, f32[24,128]{1,0:T(8,128)S(1)}) custom-call(s32[1024]{0:T(1024)S(1)} %reshape.154.cols_sm, s32[32]{0:T(128)S(1)} %get-tuple-element.61.lo_sm, s32[32]{0:T(128)S(1)} %get-tuple-element.60.hi_sm, bf16[192,24,128]{2,1,0:T(8,128)(2,1)S(1)} %bitcast.50, ...), custom_call_target="tpu_custom_call" | custom-call | tf_op jit(solution)/shard_map/flow_step/pallas_call | solution.py:88
  60.5 0.7 copy-done.9
  61.1 6.2 %exchange.4 = f32[8,24,128]{2,1,0:T(8,128)} custom-call(bf16[4,8,24,128]{3,2,1,0:T(8,128)(2,1)} %bitcast.63), custom_call_target="tpu_custom_call" | custom-call | tf_op jit(solution)/shard_map/exchange/pallas_call | solution.py:195
  67.4 1.6 multiply_bitcast_fusion.3
  69.0 3.1 %inject.5.refs_0_ = bf16[48,24,128]{2,1,0:T(8,128)(2,1)} custom-call(s32[48]{0:T(128)} %get-tuple-element.42.lo_sm, s32[48]{0:T(128)} %get-tuple-element.41.hi_sm, s32[1]{0:T(128)} %bitcast.9.slow_sm, f32[8,24,128]{2,1,0:T(8,128)} %get-tuple-element.35.disp, s32[8,1,128]{2,1,0:T(1,128)} %fusion.29.bus, bf16[24,6144]{1,0:T(8,128)(2,1)} %bitcast.67, ...), custom_call_target="tpu_custom_call" | custom-call | tf_op jit(solution)/shard_map/inject/pallas_call | solution.py:165
  72.0 12.3 %spread.4 = bf16[4,48,24,128]{3,2,1,0:T(8,128)(2,1)} custom-call(bf16[48,24,128]{2,1,0:T(8,128)(2,1)} %inject.5.refs_0_), custom_call_target="tpu_custom_call" | custom-call | tf_op jit(solution)/shard_map/spread/pallas_call | solution.py:348
  84.4 1.3 copy-done.2
  85.7 23.3 %flow_step.5 = (f32[24,4096]{1,0:T(8,128)}, bf16[32,24,128]{2,1,0:T(8,128)(2,1)S(1)}, f32[24,128]{1,0:T(8,128)S(1)}) custom-call(s32[1024]{0:T(1024)S(1)} %reshape.154.cols_sm, s32[32]{0:T(128)S(1)} %get-tuple-element.61.lo_sm, s32[32]{0:T(128)S(1)} %get-tuple-element.60.hi_sm, bf16[192,24,128]{2,1,0:T(8,128)(2,1)S(1)} %bitcast.51, ...), custom_call_target="tpu_custom_call" | custom-call | tf_op jit(solution)/shard_map/flow_step/pallas_call | solution.py:88
  109.0 0.7 copy-done.10
  109.7 6.2 %exchange.5 = f32[8,24,128]{2,1,0:T(8,128)} custom-call(bf16[4,8,24,128]{3,2,1,0:T(8,128)(2,1)} %bitcast.64), custom_call_target="tpu_custom_call" | custom-call | tf_op jit(solution)/shard_map/exchange/pallas_call | solution.py:195
  115.9 1.6 multiply_bitcast_fusion.2
  117.5 0.7 concatenate.13.refs_0_
  118.2 3.2 %inject.6.refs_1_ = bf16[48,24,128]{2,1,0:T(8,128)(2,1)} custom-call(s32[48]{0:T(128)} %get-tuple-element.42.lo_sm, s32[48]{0:T(128)} %get-tuple-element.41.hi_sm, s32[1]{0:T(128)} %bitcast.9.slow_sm, f32[8,24,128]{2,1,0:T(8,128)} %get-tuple-element.37.disp, s32[8,1,128]{2,1,0:T(1,128)} %fusion.29.bus, bf16[24,6144]{1,0:T(8,128)(2,1)} %bitcast.68, ...), custom_call_target="tpu_custom_call" | custom-call | tf_op jit(solution)/shard_map/inject/pallas_call | solution.py:165
  121.4 18.9 %spread_mean.1 = (f32[8,56,128]{2,1,0:T(8,128)}, bf16[4,48,24,128]{3,2,1,0:T(8,128)(2,1)}) custom-call(f32[8,56,128]{2,1,0:T(8,128)} %concatenate.13.refs_0_, bf16[48,24,128]{2,1,0:T(8,128)(2,1)} %inject.6.refs_1_), custom_call_target="tpu_custom_call" | custom-call | tf_op jit(solution)/shard_map/spread_mean/pallas_call | solution.py:348
  140.4 1.3 copy-done.3
  141.7 23.3 %flow_step.6 = (f32[24,4096]{1,0:T(8,128)}, bf16[32,24,128]{2,1,0:T(8,128)(2,1)S(1)}, f32[24,128]{1,0:T(8,128)S(1)}) custom-call(s32[1024]{0:T(1024)S(1)} %reshape.154.cols_sm, s32[32]{0:T(128)S(1)} %get-tuple-element.61.lo_sm, s32[32]{0:T(128)S(1)} %get-tuple-element.60.hi_sm, bf16[192,24,128]{2,1,0:T(8,128)(2,1)S(1)} %bitcast.52, ...), custom_call_target="tpu_custom_call" | custom-call | tf_op jit(solution)/shard_map/flow_step/pallas_call | solution.py:88
  165.0 0.7 copy-done.11
  165.7 6.2 %exchange.6 = f32[8,24,128]{2,1,0:T(8,128)} custom-call(bf16[4,8,24,128]{3,2,1,0:T(8,128)(2,1)} %bitcast.65), custom_call_target="tpu_custom_call" | custom-call | tf_op jit(solution)/shard_map/exchange/pallas_call | solution.py:195
  172.0 1.7 multiply_bitcast_fusion.1
  173.6 3.1 %inject.7.refs_0_ = bf16[48,24,128]{2,1,0:T(8,128)(2,1)} custom-call(s32[48]{0:T(128)} %get-tuple-element.42.lo_sm, s32[48]{0:T(128)} %get-tuple-element.41.hi_sm, s32[1]{0:T(128)} %bitcast.9.slow_sm, f32[8,24,128]{2,1,0:T(8,128)} %get-tuple-element.30.disp, s32[8,1,128]{2,1,0:T(1,128)} %fusion.29.bus, bf16[24,6144]{1,0:T(8,128)(2,1)} %bitcast.69, ...), custom_call_target="tpu_custom_call" | custom-call | tf_op jit(solution)/shard_map/inject/pallas_call | solution.py:165
  176.7 12.3 %spread.5 = bf16[4,48,24,128]{3,2,1,0:T(8,128)(2,1)} custom-call(bf16[48,24,128]{2,1,0:T(8,128)(2,1)} %inject.7.refs_0_), custom_call_target="tpu_custom_call" | custom-call | tf_op jit(solution)/shard_map/spread/pallas_call | solution.py:348
  189.1 1.3 copy-done
  190.3 23.3 %flow_step.7 = (f32[24,4096]{1,0:T(8,128)}, bf16[32,24,128]{2,1,0:T(8,128)(2,1)S(1)}, f32[24,128]{1,0:T(8,128)S(1)}) custom-call(s32[1024]{0:T(1024)S(1)} %reshape.154.cols_sm, s32[32]{0:T(128)S(1)} %get-tuple-element.61.lo_sm, s32[32]{0:T(128)S(1)} %get-tuple-element.60.hi_sm, bf16[192,24,128]{2,1,0:T(8,128)(2,1)S(1)} %bitcast.49, ...), custom_call_target="tpu_custom_call" | custom-call | tf_op jit(solution)/shard_map/flow_step/pallas_call | solution.py:88
  213.6 0.7 copy-done.8
  214.3 6.2 %exchange.7 = f32[8,24,128]{2,1,0:T(8,128)} custom-call(bf16[4,8,24,128]{3,2,1,0:T(8,128)(2,1)} %bitcast.62), custom_call_target="tpu_custom_call" | custom-call | tf_op jit(solution)/shard_map/exchange/pallas_call | solution.py:195
  220.6 1.0 multiply_bitcast_fusion
  221.5 0.7 concatenate.14.refs_0_
  222.2 17.9 %mean.1 = f32[8,56,128]{2,1,0:T(8,128)} custom-call(f32[8,56,128]{2,1,0:T(8,128)} %concatenate.14.refs_0_), custom_call_target="tpu_custom_call" | custom-call | tf_op jit(solution)/shard_map/mean/pallas_call | solution.py:348
  240.1 0.8 slice.73
  240.9 0.9 slice_divide_fusion
  241.9 2.3 fusion
  244.2 0.7 slice_bitcast_fusion
  (37 shorter events, 0.2 us)
Async XLA Ops:
  34.4 1.3 copy-start.1
  35.7 0.7 copy-start.4
  36.4 0.7 copy-start.6
  37.1 47.2 %copy-start.5 = (s32[4,8,128]{2,1,0:T(8,128)S(1)}, s32[4,8,128]{2,1,0:T(8,128)}, u32[]{:S(2)}) copy-start(s32[4,8,128]{2,1,0:T(8,128)} %gather.1) | copy-start | bytes 49156
  37.1 47.2 %copy-start.7 = (f32[4096]{0:T(1024)S(1)}, f32[4096]{0:T(1024)}, u32[]{:S(2)}) copy-start(f32[4096]{0:T(1024)} %param.12) | copy-start | bytes 49156
  60.5 0.7 copy-start.9
  84.4 1.3 copy-start.2
  85.7 30.2 %copy-start.12 = (f32[8,24,128]{2,1,0:T(8,128)S(1)}, f32[8,24,128]{2,1,0:T(8,128)}, u32[]{:S(2)}) copy-start(f32[8,24,128]{2,1,0:T(8,128)} %get-tuple-element.35.disp) | copy-start | bytes 294916
  109.0 0.7 copy-start.10
  140.4 1.3 copy-start.3
  141.7 30.2 %copy-start.15 = (f32[8,56,128]{2,1,0:T(8,128)S(1)}, f32[8,56,128]{2,1,0:T(8,128)}, u32[]{:S(2)}) copy-start(f32[8,56,128]{2,1,0:T(8,128)} %get-tuple-element.19) | copy-start | bytes 688132
  141.7 30.3 %copy-start.14 = (f32[8,24,128]{2,1,0:T(8,128)S(1)}, f32[8,24,128]{2,1,0:T(8,128)}, u32[]{:S(2)}) copy-start(f32[8,24,128]{2,1,0:T(8,128)} %get-tuple-element.37.disp) | copy-start | bytes 294916
  165.0 0.7 copy-start.11
  189.0 1.3 copy-start
  190.3 30.2 %copy-start.13 = (f32[8,24,128]{2,1,0:T(8,128)S(1)}, f32[8,24,128]{2,1,0:T(8,128)}, u32[]{:S(2)}) copy-start(f32[8,24,128]{2,1,0:T(8,128)} %get-tuple-element.30.disp) | copy-start | bytes 294916
  213.6 0.7 copy-start.8
